TPU v7x, 128 devices: a whole 4x4x4 slice. The times are simulated.
128 devices in a mesh: dp: 64 (over y_hi, z, x, core), col: 2 (over y_lo).
Axes of the slice: x: 4, y: 4 (y_hi: 2, y_lo: 2; y = y_hi * 2 + y_lo), z: 4, core: 2. Of those that a mesh axis runs over, the one named last changes fastest.
Arguments:
- tokens: bfloat16 [8192, 2048], P('dp'), may hold values from -6 to 6
- routes: int32 [8192, 8], P('dp'), may hold values from 0 to 127, all different within a row; in each aligned block of 128 rows (0 to 127, 128 to 255, ...) at most 12 rows name the same one
- probs: float32 [8192, 8], P('dp'), may hold values from 0.1 to 1
- w_gate: bfloat16 [128, 2048, 768], P('dp', None, 'col'), may hold values from -0.125 to 0.125
- w_up: bfloat16 [128, 2048, 768], P('dp', None, 'col'), may hold values from -0.125 to 0.125
- w_down: bfloat16 [128, 768, 2048], P('dp', 'col'), may hold values from -0.21875 to 0.21875
- cotangent: bfloat16 [8192, 2048], P('dp', 'col'), may hold values from -6 to 6
Outputs:
- mixed: bfloat16 [8192, 2048], P('dp', 'col')
- grad_tokens: bfloat16 [8192, 2048], P('dp', 'col')
- grad_probs: float32 [8192, 8], P('dp')
- grad_gate: bfloat16 [128, 2048, 768], P('dp', None, 'col')
- grad_up: bfloat16 [128, 2048, 768], P('dp', None, 'col')
- grad_down: bfloat16 [128, 768, 2048], P('dp', 'col')
Inputs may be any that keep to these rules, and one draw needn't show every extreme that they name: `routes`: each token names 8 different experts. Among the 128 tokens of one index of dp, no expert is named by more than 12 of them, a bound that some block reaches.
All inputs are finite; a program needn't handle non-finite values.
Results may differ from a plain program's by a relative error of at most 0.0064.
Values may be sent and summed in bfloat16 or wider, within the bound.
A program may use at most 192 MiB of HBM per device.

v0:
```python
import jax
import jax.numpy as jnp
from jax import lax
from jax.sharding import PartitionSpec as P


def body(tokens, routes, probs, w_gate, w_up, w_down, cotangent):
    tok_count, width = tokens.shape
    top_count = routes.shape[1]
    owners = lax.axis_size("dp")
    cols = lax.axis_size("col")
    local_experts = w_gate.shape[0]
    experts = local_experts * owners
    slot_cap = 3 * tok_count * top_count // (2 * experts)
    half_width = width // cols
    pair_count = tok_count * top_count
    rows_per_owner = local_experts * slot_cap
    slots = experts * slot_cap

    flat_routes = routes.reshape(-1)
    expert_ids = jnp.arange(experts, dtype=jnp.int32)
    onehot = (flat_routes[:, None] == expert_ids[None, :]).astype(jnp.int32)
    before = jnp.cumsum(onehot, axis=0) - onehot
    slot_index = jnp.sum(before * onehot, axis=1)
    flat_index = flat_routes * slot_cap + slot_index

    slot_ids = jnp.arange(slots, dtype=jnp.int32)
    match = flat_index.reshape(tok_count, top_count)[:, :, None] == slot_ids[None, None, :]
    weight = jnp.sum(jnp.where(match, probs[:, :, None], 0.0), axis=1)
    taken = jnp.any(match, axis=1)
    picker = taken.astype(jnp.bfloat16)
    weight_hi = weight.astype(jnp.bfloat16)
    weight_lo = (weight - weight_hi.astype(jnp.float32)).astype(jnp.bfloat16)
    prob_of_slot = jnp.sum(weight, axis=0)

    both = ("dp", "col")

    col_me = lax.axis_index("col")
    tok_half = lax.dynamic_slice_in_dim(tokens, col_me * half_width, half_width, axis=1)
    tok_rows = jnp.einsum("ts,td->sd", picker, tok_half, preferred_element_type=jnp.float32)
    cot_rows = jnp.einsum("ts,td->sd", picker, cotangent, preferred_element_type=jnp.float32)

    def dispatch(rows_half):
        spread = jnp.broadcast_to(
            rows_half.reshape(owners, 1, rows_per_owner, half_width),
            (owners, cols, rows_per_owner, half_width),
        ).reshape(owners * cols, rows_per_owner, half_width)
        got = lax.all_to_all(spread, both, 0, 0, tiled=True)
        return got.reshape(owners, cols, rows_per_owner, half_width)

    row_block = dispatch(tok_rows.astype(jnp.bfloat16))
    d_out = dispatch((prob_of_slot[:, None] * cot_rows).astype(jnp.bfloat16))
    w_gate_h = w_gate.reshape(local_experts, cols, half_width, -1)
    w_up_h = w_up.reshape(local_experts, cols, half_width, -1)
    w_down_h = w_down.reshape(local_experts, w_down.shape[1], cols, half_width)

    expert_of_row = jnp.arange(rows_per_owner, dtype=jnp.int32) // slot_cap
    own = (expert_of_row[:, None] == jnp.arange(local_experts, dtype=jnp.int32)[None, :])[
        None, :, :, None
    ]

    def per_half(table):
        return jnp.broadcast_to(
            table.reshape(tok_count, owners, 1, rows_per_owner),
            (tok_count, owners, cols, rows_per_owner),
        )

    def send_back(halves):
        part = jnp.stack([h.astype(jnp.bfloat16) for h in halves], axis=1)
        got = lax.all_to_all(
            part.reshape(owners * cols, rows_per_owner, half_width), both, 0, 0, tiled=True
        )
        return got.reshape(owners, cols, rows_per_owner, half_width)

    def flat(got):
        return got.reshape(owners * cols * rows_per_owner, half_width)

    def combine(table, got):
        lhs = per_half(table).reshape(tok_count, owners * cols * rows_per_owner)
        return jnp.dot(lhs, flat(got), preferred_element_type=jnp.float32)

    def halves_of(ref, axis):
        return [lax.slice_in_dim(ref, j * half_width, (j + 1) * half_width, axis=axis) for j in range(cols)]

    gate_acts = jnp.einsum("scrd,lcdh->srlh", row_block, w_gate_h, preferred_element_type=jnp.float32)
    up_acts = jnp.einsum("scrd,lcdh->srlh", row_block, w_up_h, preferred_element_type=jnp.float32)
    gate_acts = jnp.where(own, gate_acts, 0.0)
    up_acts = jnp.where(own, up_acts, 0.0)
    sigmoid_g = jax.nn.sigmoid(gate_acts)
    silu_g = gate_acts * sigmoid_g
    hidden = (silu_g * up_acts).astype(jnp.bfloat16)
    out_halves = [
        jnp.einsum("srlh,lhd->srd", hidden, w, preferred_element_type=jnp.float32)
        for w in halves_of(w_down, 2)
    ]
    d_out, out_halves = lax.optimization_barrier((d_out, out_halves))
    got_out = send_back(out_halves)
    stacked = jnp.broadcast_to(
        jnp.stack([weight_hi, weight_lo]).reshape(2, tok_count, owners, 1, rows_per_owner),
        (2, tok_count, owners, cols, rows_per_owner),
    )
    both_parts = jnp.dot(
        stacked.reshape(2 * tok_count, owners * cols * rows_per_owner),
        flat(got_out),
        preferred_element_type=jnp.float32,
    )
    mixed = (both_parts[:tok_count] + both_parts[tok_count:]).astype(jnp.bfloat16)
    dots = lax.dot_general(
        cotangent, flat(got_out), (((1,), (1,)), ((), ())), preferred_element_type=jnp.float32
    ).reshape(tok_count, owners, cols, rows_per_owner)
    dots = jnp.sum(dots, axis=2).reshape(tok_count, 1, slots)
    prob_part = jnp.sum(jnp.where(match, dots, 0.0), axis=2)

    grad_down = jnp.einsum(
        "srlh,scrd->lhcd", hidden, d_out, preferred_element_type=jnp.float32
    ).astype(jnp.bfloat16).reshape(w_down.shape)
    d_hidden = jnp.einsum("scrd,lhcd->srlh", d_out, w_down_h, preferred_element_type=jnp.float32)
    d_hidden = jnp.where(own, d_hidden, 0.0)
    d_gate = (d_hidden * up_acts * sigmoid_g * (1.0 + gate_acts * (1.0 - sigmoid_g))).astype(
        jnp.bfloat16
    )
    d_up = (d_hidden * silu_g).astype(jnp.bfloat16)
    grad_gate = jnp.einsum(
        "scrd,srlh->lcdh", row_block, d_gate, preferred_element_type=jnp.float32
    ).astype(jnp.bfloat16).reshape(w_gate.shape)
    grad_up = jnp.einsum(
        "scrd,srlh->lcdh", row_block, d_up, preferred_element_type=jnp.float32
    ).astype(jnp.bfloat16).reshape(w_up.shape)
    got_grad = send_back(
        [
            jnp.einsum("srlh,ldh->srd", d_gate, wg, preferred_element_type=jnp.float32)
            + jnp.einsum("srlh,ldh->srd", d_up, wu, preferred_element_type=jnp.float32)
            for wg, wu in zip(halves_of(w_gate, 1), halves_of(w_up, 1))
        ]
    )
    grad_tokens = combine(picker, got_grad).astype(jnp.bfloat16)
    prob_part, mixed = lax.optimization_barrier((prob_part, mixed))
    grad_probs = lax.psum(prob_part, "col")
    return (mixed, grad_tokens, grad_probs, grad_gate, grad_up, grad_down)


def solution(mesh):
    return jax.shard_map(
        body,
        mesh=mesh,
        in_specs=(
            P("dp", None),
            P("dp", None),
            P("dp", None),
            P("dp", None, "col"),
            P("dp", None, "col"),
            P("dp", "col", None),
            P("dp", "col"),
        ),
        out_specs=(
            P("dp", "col"),
            P("dp", "col"),
            P("dp", None),
            P("dp", None, "col"),
            P("dp", None, "col"),
            P("dp", "col", None),
        ),
        check_vma=False,
    )
```

profile of v0, /device:TPU:82, one launch (start us, length us, event | category | flops | bytes accessed | tf_op | source)
XLA Modules:
  0.0 391.0 jit_solution(977694177589642852)
XLA Ops:
  2.9 3.1 fusion.11
  7.1 3.5 broadcast_in_dim.87
  10.5 10.3 %all-to-all-start.1 = ((bf16[128,24,1024]{2,1,0:T(8,128)(2,1)}), bf16[128,24,1024]{2,1,0:T(8,128)(2,1)}, u32[]{:S(2)}, u32[]{:S(2)}) async-start(bf16[128,24,1024]{2,1,0:T(8,128)(2,1)} %bitcast.215), calls=%async_computation.1 | async-start | bytes 12582912 | tf_op jit(solution)/shard_map/all_to_all | solution.py:48
  26.2 75.6 %all-to-all-done.1 = bf16[128,24,1024]{2,1,0:T(8,128)(2,1)} async-done(((bf16[128,24,1024]{2,1,0:T(8,128)(2,1)}), bf16[128,24,1024]{2,1,0:T(8,128)(2,1)}, u32[]{:S(2)}, u32[]{:S(2)}) %all-to-all-start.1) | async-done | bytes 6291488 | tf_op jit(solution)/shard_map/all_to_all | solution.py:48
  101.7 5.5 %broadcast_in_dim.84 = bf16[64,2,24,1024]{3,2,1,0:T(8,128)(2,1)} broadcast(bf16[64,24,1024]{2,1,0:T(8,128)(2,1)} %bitcast.218), dimensions={0,2,3} | broadcast | bytes 9437184 | tf_op jit(solution)/shard_map/broadcast_in_dim | solution.py:44
  107.2 10.0 %all-to-all-start = ((bf16[128,24,1024]{2,1,0:T(8,128)(2,1)}), bf16[128,24,1024]{2,1,0:T(8,128)(2,1)}, u32[]{:S(2)}, u32[]{:S(2)}) async-start(bf16[128,24,1024]{2,1,0:T(8,128)(2,1)} %bitcast.214), calls=%async_computation | async-start | bytes 12582912 | tf_op jit(solution)/shard_map/all_to_all | solution.py:48
  120.4 7.3 %fusion.60 = f32[64,24,2,384,1]{3,1,4,2,0:T(8,128)S(1)} fusion(bf16[64,2,24,1024,1]{3,2,1,4,0:T(8,128)(2,1)} %bitcast.10, bf16[2,2,1024,384,1]{3,2,1,0,4:T(8,128)(2,1)S(1)} %bitcast.230), kind=kOutput, calls=%fused_computation.88 | convolution fusion | flops 4831838208 | bytes 14155776 | tf_op jit(solution)/shard_map/scrd,lcdh->srlh/dot_general | solution.py:85
  127.8 13.7 %multiply_convert_fusion.3 = (bf16[64,24,2,384]{3,1,2,0:T(8,128)(2,1)S(1)}, f32[64,24,2,384,1]{3,1,4,2,0:T(8,128)}) fusion(pred[24,2]{0,1:T(4,128)(4,1)S(1)} %iota_compare_fusion.4, f32[64,24,2,384,1]{3,1,4,2,0:T(8,128)S(1)} %fusion.60, bf16[64,2,24,1024,1]{3,2,1,4,0:T(8,128)(2,1)} %bitcast.10, bf16[2,2,1024,384,1]{3,2,1,0,4:T(8,128)(2,1)S(1)} %bitcast.231), kind=kOutput, calls=%fused_computation.31 | convolution fusion | flops 4841275392 | bytes 21233712 | tf_op jit(solution)/shard_map/scrd,lcdh->srlh/dot_general | solution.py:86
  141.6 4.0 %convolution_bitcast_fusion = bf16[64,24,1024]{2,1,0:T(8,128)(2,1)} fusion(bf16[64,24,2,384]{3,1,2,0:T(8,128)(2,1)S(1)} %get-tuple-element.40, bf16[2,384,2048]{2,1,0:T(8,128)(2,1)S(1)} %copy-done.9), kind=kOutput, calls=%fused_computation.43 | convolution fusion | flops 2415919104 | bytes 7077888 | tf_op jit(solution)/shard_map/srlh,lhd->srd/dot_general | solution.py:93
  145.5 4.0 %convolution_bitcast_fusion.1 = bf16[64,24,1024]{2,1,0:T(8,128)(2,1)} fusion(bf16[64,24,2,384]{3,1,2,0:T(8,128)(2,1)S(1)} %get-tuple-element.40, bf16[2,384,2048]{2,1,0:T(8,128)(2,1)S(1)} %copy-done.9), kind=kOutput, calls=%fused_computation.44 | convolution fusion | flops 2415919104 | bytes 7077888 | tf_op jit(solution)/shard_map/srlh,lhd->srd/dot_general | solution.py:93
  149.5 46.5 %all-to-all-done = bf16[128,24,1024]{2,1,0:T(8,128)(2,1)} async-done(((bf16[128,24,1024]{2,1,0:T(8,128)(2,1)}), bf16[128,24,1024]{2,1,0:T(8,128)(2,1)}, u32[]{:S(2)}, u32[]{:S(2)}) %all-to-all-start) | async-done | bytes 6291488 | tf_op jit(solution)/shard_map/all_to_all | solution.py:48
  196.0 3.4 pad_maximum_fusion
  199.4 3.3 copy.76
  202.7 10.1 %all-to-all-start.2 = ((bf16[128,24,1024]{2,1,0:T(8,128)(2,1)}), bf16[128,24,1024]{2,1,0:T(8,128)(2,1)}, u32[]{:S(2)}, u32[]{:S(2)}) async-start(bf16[128,24,1024]{2,1,0:T(8,128)(2,1)} %bitcast.212), calls=%async_computation.2 | async-start | bytes 12582912 | tf_op jit(solution)/shard_map/all_to_all | solution.py:70
  212.8 9.3 %bitcast_convert_fusion = bf16[2,384,2,1024]{3,1,2,0:T(8,128)(2,1)} fusion(bf16[64,2,24,1024]{3,2,1,0:T(8,128)(2,1)} %bitcast.5, bf16[64,24,2,384]{3,1,2,0:T(8,128)(2,1)S(1)} %get-tuple-element.40), kind=kOutput, calls=%fused_computation.6 | convolution fusion | flops 4833411072 | bytes 11796480 | tf_op jit(solution)/shard_map/srlh,scrd->lhcd/dot_general | solution.py:114
  222.1 4.6 %copy.91 = bf16[2,384,2,1024]{1,3,2,0:T(8,128)(2,1)} copy(bf16[2,384,2,1024]{3,1,2,0:T(8,128)(2,1)} %bitcast_convert_fusion) | data formatting | bytes 6291456 | tf_op jit(solution)/shard_map/convert_element_type | solution.py:116
  226.7 4.6 %copy.93 = bf16[2,384,2048]{2,1,0:T(8,128)(2,1)} copy(bf16[2,384,2048]{1,2,0:T(8,128)(2,1)} %bitcast.217) | data formatting | bytes 6291456
  231.4 13.6 %multiply_convert_fusion.1 = (bf16[64,24,2,384]{3,1,2,0:T(8,128)(2,1)S(1)}, bf16[64,24,2,384]{3,1,2,0:T(8,128)(2,1)S(1)}) fusion(pred[24,2]{0,1:T(4,128)(4,1)S(1)} %iota_compare_fusion.4, f32[64,24,2,384,1]{3,1,4,2,0:T(8,128)} %copy-done.16, f32[64,24,2,384,1]{3,1,4,2,0:T(8,128)} %get-tuple-element.41, bf16[2,48,2,8,1024]{4,3,2,1,0:T(8,128)(2,1)} %bitcast.229, ...), kind=kOutput, calls=%fused_computation.29 | convolution fusion | flops 4850712576 | bytes 23593008 | tf_op jit(solution)/shard_map/scrd,lhcd->srlh/dot_general | solution.py:117
  246.4 9.3 %fusion.17 = bf16[2,2,1024,384]{2,3,1,0:T(8,128)(2,1)} fusion(bf16[64,2,24,1024]{3,2,1,0:T(8,128)(2,1)} %bitcast.8, bf16[64,24,2,384]{3,1,2,0:T(8,128)(2,1)S(1)} %get-tuple-element.39), kind=kOutput, calls=%fused_computation.37 | convolution fusion | flops 4833411072 | bytes 11796480 | tf_op jit(solution)/shard_map/scrd,srlh->lcdh/dot_general | solution.py:123
  255.7 5.0 %copy.85 = bf16[2,2,1024,384]{3,2,1,0:T(8,128)(2,1)} copy(bf16[2,2,1024,384]{2,3,1,0:T(8,128)(2,1)} %fusion.17) | data formatting | bytes 6291456 | tf_op jit(solution)/shard_map/convert_element_type | solution.py:125
  260.7 5.0 %fusion.39 = f32[64,24,1024,1]{2,1,3,0:T(8,128)S(1)} fusion(bf16[64,24,2,384]{3,1,2,0:T(8,128)(2,1)} %copy-done.14, bf16[2,2048,384]{2,1,0:T(8,128)(2,1)} %param.10), kind=kOutput, calls=%fused_computation.52 | convolution fusion | flops 2415919104 | bytes 10223616 | tf_op jit(solution)/shard_map/srlh,ldh->srd/dot_general | solution.py:131
  268.5 3.1 fusion.16
  271.6 3.1 fusion.15
  275.4 3.4 copy.82
  278.8 12.8 %all-to-all-done.2 = bf16[128,24,1024]{2,1,0:T(8,128)(2,1)} async-done(((bf16[128,24,1024]{2,1,0:T(8,128)(2,1)}), bf16[128,24,1024]{2,1,0:T(8,128)(2,1)}, u32[]{:S(2)}, u32[]{:S(2)}) %all-to-all-start.2) | async-done | bytes 6291488 | tf_op jit(solution)/shard_map/all_to_all | solution.py:70
  291.6 10.0 %all-to-all-start.3 = ((bf16[128,24,1024]{2,1,0:T(8,128)(2,1)}), bf16[128,24,1024]{2,1,0:T(8,128)(2,1)}, u32[]{:S(2)}, u32[]{:S(2)}) async-start(bf16[128,24,1024]{2,1,0:T(8,128)(2,1)} %bitcast.213), calls=%async_computation.3 | async-start | bytes 12582912 | tf_op jit(solution)/shard_map/all_to_all | solution.py:70
  301.6 9.3 %fusion.18 = bf16[2,2,1024,384]{2,3,1,0:T(8,128)(2,1)} fusion(bf16[64,2,24,1024]{3,2,1,0:T(8,128)(2,1)} %bitcast.8, bf16[64,24,2,384]{3,1,2,0:T(8,128)(2,1)S(1)} %get-tuple-element.38), kind=kOutput, calls=%fused_computation.38 | convolution fusion | flops 4833411072 | bytes 11796480 | tf_op jit(solution)/shard_map/scrd,srlh->lcdh/dot_general | solution.py:126
  310.9 4.7 %copy.88 = bf16[2,2,1024,384]{3,2,1,0:T(8,128)(2,1)} copy(bf16[2,2,1024,384]{2,3,1,0:T(8,128)(2,1)} %fusion.18) | data formatting | bytes 6291456 | tf_op jit(solution)/shard_map/convert_element_type | solution.py:128
  315.6 4.6 %fusion.61 = f32[3072,128]{1,0:T(8,128)S(1)} fusion(bf16[3072,1024]{1,0:T(8,128)(2,1)} %bitcast.30, bf16[128,1024]{1,0:T(8,128)(2,1)S(1)} %copy-done.6), kind=kOutput, calls=%fused_computation.89 | convolution fusion | flops 805306368 | bytes 8126464 | tf_op jit(solution)/shard_map/dot_general | solution.py:108
  322.6 4.7 %fusion.35 = f32[256,1024]{1,0:T(8,128)S(1)} fusion(bf16[3072,1024]{1,0:T(8,128)(2,1)} %bitcast.30, bf16[384,8,2,128]{3,2,1,0:T(2,128)(2,1)S(1)} %bitcast.216), kind=kOutput, calls=%fused_computation.48 | convolution fusion | flops 1610612736 | bytes 8912896 | tf_op jit(solution)/shard_map/dot_general | solution.py:102
  329.0 56.5 %psum.7 = f32[128,8]{1,0:T(8,128)S(1)} all-reduce(f32[128,8]{1,0:T(8,128)S(1)} %select_reduce_fusion.2), channel_id=1, replica_groups=mesh['dp'=64,'col'=2] {'col'}, use_global_device_ids=true, to_apply=%region_8.9 | all-reduce | flops 1024 | bytes 8192 | tf_op jit(solution)/shard_map/psum | solution.py:138
  386.2 4.6 %convolution_convert_fusion.1 = bf16[128,1024]{1,0:T(8,128)(2,1)} fusion(bf16[128,3072]{0,1:T(8,128)(2,1)S(1)} %bitcast.222, bf16[3072,1024]{1,0:T(8,128)(2,1)} %bitcast.58), kind=kOutput, calls=%fused_computation.65 | convolution fusion | flops 805437440 | bytes 7340032 | tf_op jit(solution)/shard_map/dot_general | solution.py:80
  (71 shorter events, 21.1 us)
Async XLA Ops:
  0.6 5.4 %copy-start = (bf16[128,2048]{1,0:T(8,128)(2,1)S(1)}, bf16[128,2048]{1,0:T(8,128)(2,1)}, u32[]{:S(2)}) copy-start(bf16[128,2048]{1,0:T(8,128)(2,1)} %param.7) | copy-start | bytes 1572868
  0.6 2.1 copy-start.7
  2.8 18.1 %copy-start.3 = (s32[128,8]{1,0:T(8,128)}, s32[128,8]{1,0:T(8,128)S(1)}, u32[]{:S(2)}) copy-start(s32[128,8]{1,0:T(8,128)S(1)} %copy.74) | copy-start | bytes 12292
  10.5 10.3 %copy-start.8 = (f32[128,8]{0,1:T(8,128)S(1)}, f32[128,8]{0,1:T(8,128)}, u32[]{:S(2)}) copy-start(f32[128,8]{0,1:T(8,128)} %param.9) | copy-start | bytes 12292
  10.5 12.9 %copy-start.5 = (bf16[128,1024]{1,0:T(8,128)(2,1)S(1)}, bf16[128,1024]{1,0:T(8,128)(2,1)}, u32[]{:S(2)}) copy-start(bf16[128,1024]{1,0:T(8,128)(2,1)} %param.13) | copy-start | bytes 786436
  10.5 91.2 %all-to-all-start.1 = ((bf16[128,24,1024]{2,1,0:T(8,128)(2,1)}), bf16[128,24,1024]{2,1,0:T(8,128)(2,1)}, u32[]{:S(2)}, u32[]{:S(2)}) async-start(bf16[128,24,1024]{2,1,0:T(8,128)(2,1)} %bitcast.215), calls=%async_computation.1 | async-start | bytes 12582912 | tf_op jit(solution)/shard_map/all_to_all | solution.py:48
  107.2 88.8 %all-to-all-start = ((bf16[128,24,1024]{2,1,0:T(8,128)(2,1)}), bf16[128,24,1024]{2,1,0:T(8,128)(2,1)}, u32[]{:S(2)}, u32[]{:S(2)}) async-start(bf16[128,24,1024]{2,1,0:T(8,128)(2,1)} %bitcast.214), calls=%async_computation | async-start | bytes 12582912 | tf_op jit(solution)/shard_map/all_to_all | solution.py:48
  118.5 1.9 copy-start.10
  120.4 7.4 %copy-start.12 = (bf16[2,2048,384]{2,1,0:T(8,128)(2,1)S(1)}, bf16[2,2048,384]{2,1,0:T(8,128)(2,1)}, u32[]{:S(2)}) copy-start(bf16[2,2048,384]{2,1,0:T(8,128)(2,1)} %param.11) | copy-start | bytes 9437188
  127.8 13.8 %copy-start.16 = (f32[64,24,2,384,1]{3,1,4,2,0:T(8,128)}, f32[64,24,2,384,1]{3,1,4,2,0:T(8,128)S(1)}, u32[]{:S(2)}) copy-start(f32[64,24,2,384,1]{3,1,4,2,0:T(8,128)S(1)} %fusion.60) | copy-start | bytes 14155780
  127.8 13.8 %copy-start.9 = (bf16[2,384,2048]{2,1,0:T(8,128)(2,1)S(1)}, bf16[2,384,2048]{2,1,0:T(8,128)(2,1)}, u32[]{:S(2)}) copy-start(bf16[2,384,2048]{2,1,0:T(8,128)(2,1)} %param.12) | copy-start | bytes 9437188
  202.7 88.8 %all-to-all-start.2 = ((bf16[128,24,1024]{2,1,0:T(8,128)(2,1)}), bf16[128,24,1024]{2,1,0:T(8,128)(2,1)}, u32[]{:S(2)}, u32[]{:S(2)}) async-start(bf16[128,24,1024]{2,1,0:T(8,128)(2,1)} %bitcast.212), calls=%async_computation.2 | async-start | bytes 12582912 | tf_op jit(solution)/shard_map/all_to_all | solution.py:70
  245.0 1.4 copy-start.14
  260.7 5.0 %copy-start.11 = (bf16[2,2048,384]{2,1,0:T(8,128)(2,1)S(1)}, bf16[2,2048,384]{2,1,0:T(8,128)(2,1)}, u32[]{:S(2)}) copy-start(bf16[2,2048,384]{2,1,0:T(8,128)(2,1)} %param.10) | copy-start | bytes 9437188
  260.7 5.0 %copy-start.15 = (bf16[64,24,2,384]{3,1,2,0:T(8,128)(2,1)S(1)}, bf16[64,24,2,384]{3,1,2,0:T(8,128)(2,1)}, u32[]{:S(2)}) copy-start(bf16[64,24,2,384]{3,1,2,0:T(8,128)(2,1)} %copy-done.14) | copy-start | bytes 7077892
  265.7 2.7 copy-start.13
  291.6 94.5 %all-to-all-start.3 = ((bf16[128,24,1024]{2,1,0:T(8,128)(2,1)}), bf16[128,24,1024]{2,1,0:T(8,128)(2,1)}, u32[]{:S(2)}, u32[]{:S(2)}) async-start(bf16[128,24,1024]{2,1,0:T(8,128)(2,1)} %bitcast.213), calls=%async_computation.3 | async-start | bytes 12582912 | tf_op jit(solution)/shard_map/all_to_all | solution.py:70
  310.9 4.7 %copy-start.6 = (bf16[128,1024]{1,0:T(8,128)(2,1)S(1)}, bf16[128,1024]{1,0:T(8,128)(2,1)}, u32[]{:S(2)}) copy-start(bf16[128,1024]{1,0:T(8,128)(2,1)} %param.13) | copy-start | bytes 786436
  322.6 5.5 %copy-start.4 = (s32[128,8]{1,0:T(8,128)S(1)}, s32[128,8]{1,0:T(8,128)}, u32[]{:S(2)}) copy-start(s32[128,8]{1,0:T(8,128)} %copy-done.3) | copy-start | bytes 12292
  322.6 63.5 %copy-start.2 = (bf16[128,1536]{0,1:T(8,128)(2,1)S(1)}, bf16[128,1536]{0,1:T(8,128)(2,1)}, u32[]{:S(2)}) copy-start(bf16[128,1536]{0,1:T(8,128)(2,1)} %copy.80) | copy-start | bytes 1179652
  386.2 4.6 %copy-start.1 = (bf16[128,2048]{1,0:T(8,128)(2,1)S(1)}, bf16[128,2048]{1,0:T(8,128)(2,1)}, u32[]{:S(2)}) copy-start(bf16[128,2048]{1,0:T(8,128)(2,1)} %param.7) | copy-start | bytes 1572868
where the time goes:
time: 399 us; the launch traced here: 391 us
  waiting for transfers between devices  135 us (34%)
  matrix products  102 us (26%)
  blocking collectives  56.5 us (14%)
  local copies, waits for them, and re-layouts  43.6 us (11%)
  starting transfers between devices  40.4 us (10%)
  other arithmetic  12.3 us (3%)
    all_to_all x2, waiting for transfers between devices, dispatch(): got = lax.all_to_all(spread, both, 0, 0, tiled=True)  122 us
    psum x1, blocking collectives, body(): grad_probs = lax.psum(prob_part, 'col')  56.5 us
    all_to_all x2, starting transfers between devices, dispatch(): got = lax.all_to_all(spread, both, 0, 0, tiled=True)  20.3 us
    all_to_all x2, starting transfers between devices, send_back(): lax.all_to_all(part.reshape(owners * cols, rows_per_owner, half_width), b...  20.1 us
    dot_general x1, matrix products, body(): jnp.einsum('scrd,lcdh->srlh', row_block, w_up_h, preferred_element_type=j...  13.7 us
    dot_general x1, matrix products, body(): jnp.einsum('scrd,lhcd->srlh', d_out, w_down_h, preferred_element_type=jnp...  13.6 us
    all_to_all x2, waiting for transfers between devices, send_back(): lax.all_to_all(part.reshape(owners * cols, rows_per_owner, half_width), b...  12.8 us
    dot_general x1, matrix products, body(): jnp.einsum('scrd,srlh->lcdh', row_block, d_up, preferred_element_type=jnp...  9.31 us
  transfers between devices with their start and end apart: 4, of which 3 were waited for; matrix products, arithmetic and copies ran while one was open for 33% of the time, Pallas kernels for 0%

commit v1 on v0

--- a/solution.py
+++ b/solution.py
@@ -40,16 +40,24 @@
     tok_rows = jnp.einsum("ts,td->sd", picker, tok_half, preferred_element_type=jnp.float32)
     cot_rows = jnp.einsum("ts,td->sd", picker, cotangent, preferred_element_type=jnp.float32)
 
-    def dispatch(rows_half):
-        spread = jnp.broadcast_to(
+    def spread(rows_half):
+        return jnp.broadcast_to(
             rows_half.reshape(owners, 1, rows_per_owner, half_width),
             (owners, cols, rows_per_owner, half_width),
         ).reshape(owners * cols, rows_per_owner, half_width)
-        got = lax.all_to_all(spread, both, 0, 0, tiled=True)
+
+    def dispatch(sent):
+        got = lax.all_to_all(sent, both, 0, 0, tiled=True)
         return got.reshape(owners, cols, rows_per_owner, half_width)
 
-    row_block = dispatch(tok_rows.astype(jnp.bfloat16))
-    d_out = dispatch((prob_of_slot[:, None] * cot_rows).astype(jnp.bfloat16))
+    tok_sent, cot_sent = lax.optimization_barrier(
+        (
+            spread(tok_rows.astype(jnp.bfloat16)),
+            spread((prob_of_slot[:, None] * cot_rows).astype(jnp.bfloat16)),
+        )
+    )
+    row_block = dispatch(tok_sent)
+    d_out = dispatch(cot_sent)
     w_gate_h = w_gate.reshape(local_experts, cols, half_width, -1)
     w_up_h = w_up.reshape(local_experts, cols, half_width, -1)
     w_down_h = w_down.reshape(local_experts, w_down.shape[1], cols, half_width)

time: 399 us -> 389 us (0.975)
  blocking collectives: 56.5 us -> 137 us
  waiting for transfers between devices: 135 us -> 67.5 us
  matrix products: 102 us -> 92.1 us
  starting transfers between devices: 40.4 us -> 31.8 us
    all_to_all x0 -> x1, blocking collectives: none -> 80.2 us  [dispatch(): got = lax.all_to_all(sent, both, 0, 0, tiled=True)]
    all_to_all x2 -> x1, waiting for transfers between devices: 122 us -> 52.4 us  [dispatch(): got = lax.all_to_all(sent, both, 0, 0, tiled=True)]
    all_to_all x2 -> x1, starting transfers between devices: 20.3 us -> 11.7 us  [dispatch(): got = lax.all_to_all(sent, both, 0, 0, tiled=True)]
    dot_general x1, matrix products: 13.7 us -> 7.4 us  [body(): jnp.einsum('scrd,lcdh->srlh', row_block, w_up_h, preferred_element_type=j...]
    broadcast_in_dim x2, local copies, waits for them, and re-layouts: 8.95 us -> 4.37 us  [spread(): jnp.broadcast_to(rows_half.reshape(owners, 1, rows_per_owner, half_width)...]
    unnamed x38 -> x48, local copies, waits for them, and re-layouts: 7.75 us -> 8.57 us
  transfers between devices with their start and end apart: 4 -> 3, of which waited for: 3 -> 2; matrix products, arithmetic and copies ran while one was open for 33% -> 30% of each run, Pallas kernels for 0% -> 0%
where the time goes in v1:
time: 389 us; the launch traced here: 382 us
  blocking collectives  137 us (35%)
  matrix products  92.1 us (24%)
  waiting for transfers between devices  67.5 us (17%)
  local copies, waits for them, and re-layouts  39.7 us (10%)
  starting transfers between devices  31.8 us (8%)
  other arithmetic  12.3 us (3%)
    all_to_all x1, blocking collectives, dispatch(): got = lax.all_to_all(sent, both, 0, 0, tiled=True)  80.2 us
    psum x1, blocking collectives, body(): grad_probs = lax.psum(prob_part, 'col')  56.5 us
    all_to_all x1, waiting for transfers between devices, dispatch(): got = lax.all_to_all(sent, both, 0, 0, tiled=True)  52.4 us
    all_to_all x2, starting transfers between devices, send_back(): lax.all_to_all(part.reshape(owners * cols, rows_per_owner, half_width), b...  20.1 us
    all_to_all x2, waiting for transfers between devices, send_back(): lax.all_to_all(part.reshape(owners * cols, rows_per_owner, half_width), b...  15.1 us
    dot_general x1, matrix products, body(): jnp.einsum('scrd,lhcd->srlh', d_out, w_down_h, preferred_element_type=jnp...  14.8 us
    all_to_all x1, starting transfers between devices, dispatch(): got = lax.all_to_all(sent, both, 0, 0, tiled=True)  11.7 us
    dot_general x1, matrix products, body(): jnp.einsum('srlh,scrd->lhcd', hidden, d_out, preferred_element_type=jnp.f...  9.29 us
  transfers between devices with their start and end apart: 3, of which 2 were waited for; matrix products, arithmetic and copies ran while one was open for 30% of the time, Pallas kernels for 0%

profile of v1, /device:TPU:82, one launch (start us, length us, event | category | flops | bytes accessed | tf_op | source)
XLA Modules:
  0.0 381.7 jit_solution(2753015450887470145)
XLA Ops:
  3.7 3.1 fusion.11
  6.8 2.5 select_reduce_fusion
  11.4 3.4 broadcast_in_dim.86
  15.8 80.2 %all_to_all.20 = bf16[128,24,1024]{2,1,0:T(8,128)(2,1)} all-to-all(bf16[128,24,1024]{2,1,0:T(8,128)(2,1)S(1)} %bitcast.215), channel_id=1, replica_groups=mesh['dp'=64,'col'=2] {'dp','col'}, dimensions={0} | all-to-all | bytes 12582912 | tf_op jit(solution)/shard_map/all_to_all | solution.py:50
  95.9 11.7 %all-to-all-start = ((bf16[128,24,1024]{2,1,0:T(8,128)(2,1)}), bf16[128,24,1024]{2,1,0:T(8,128)(2,1)}, u32[]{:S(2)}, u32[]{:S(2)}) async-start(bf16[128,24,1024]{2,1,0:T(8,128)(2,1)} %bitcast.212), calls=%async_computation | async-start | bytes 12582912 | tf_op jit(solution)/shard_map/all_to_all | solution.py:50
  110.9 7.7 %fusion.60 = f32[64,24,2,384,1]{3,1,4,2,0:T(8,128)S(1)} fusion(bf16[64,2,24,1024,1]{3,2,1,4,0:T(8,128)(2,1)} %bitcast.221, bf16[2,2,1024,384,1]{3,2,1,0,4:T(8,128)(2,1)S(1)} %bitcast.238), kind=kOutput, calls=%fused_computation.88 | convolution fusion | flops 4831838208 | bytes 14155776 | tf_op jit(solution)/shard_map/scrd,lcdh->srlh/dot_general | solution.py:93
  118.7 7.4 %multiply_convert_fusion.3 = (bf16[64,24,2,384]{3,1,2,0:T(8,128)(2,1)S(1)}, f32[64,24,2,384,1]{3,1,4,2,0:T(8,128)}) fusion(pred[24,2]{0,1:T(4,128)(4,1)S(1)} %iota_compare_fusion.4, f32[64,24,2,384,1]{3,1,4,2,0:T(8,128)S(1)} %fusion.60, bf16[64,2,24,1024,1]{3,2,1,4,0:T(8,128)(2,1)S(1)} %bitcast.225, bf16[2,2,1024,384,1]{3,2,1,0,4:T(8,128)(2,1)S(1)} %bitcast.239), kind=kOutput, calls=%fused_computation.31 | convolution fusion | flops 4841275392 | bytes 21233712 | tf_op jit(solution)/shard_map/scrd,lcdh->srlh/dot_general | solution.py:94
  126.1 4.0 %convolution_bitcast_fusion = bf16[64,24,1024]{2,1,0:T(8,128)(2,1)} fusion(bf16[64,24,2,384]{3,1,2,0:T(8,128)(2,1)S(1)} %get-tuple-element.44, bf16[2,384,2048]{2,1,0:T(8,128)(2,1)S(1)} %copy-done.8), kind=kOutput, calls=%fused_computation.43 | convolution fusion | flops 2415919104 | bytes 7077888 | tf_op jit(solution)/shard_map/srlh,lhd->srd/dot_general | solution.py:101
  130.1 4.0 %convolution_bitcast_fusion.1 = bf16[64,24,1024]{2,1,0:T(8,128)(2,1)} fusion(bf16[64,24,2,384]{3,1,2,0:T(8,128)(2,1)S(1)} %get-tuple-element.44, bf16[2,384,2048]{2,1,0:T(8,128)(2,1)S(1)} %copy-done.8), kind=kOutput, calls=%fused_computation.44 | convolution fusion | flops 2415919104 | bytes 7077888 | tf_op jit(solution)/shard_map/srlh,lhd->srd/dot_general | solution.py:101
  134.0 52.4 %all-to-all-done = bf16[128,24,1024]{2,1,0:T(8,128)(2,1)} async-done(((bf16[128,24,1024]{2,1,0:T(8,128)(2,1)}), bf16[128,24,1024]{2,1,0:T(8,128)(2,1)}, u32[]{:S(2)}, u32[]{:S(2)}) %all-to-all-start) | async-done | bytes 6291488 | tf_op jit(solution)/shard_map/all_to_all | solution.py:50
  186.5 3.4 pad_maximum_fusion
  189.9 3.3 copy.76
  193.2 10.0 %all-to-all-start.2 = ((bf16[128,24,1024]{2,1,0:T(8,128)(2,1)}), bf16[128,24,1024]{2,1,0:T(8,128)(2,1)}, u32[]{:S(2)}, u32[]{:S(2)}) async-start(bf16[128,24,1024]{2,1,0:T(8,128)(2,1)} %bitcast.213), calls=%async_computation.2 | async-start | bytes 12582912 | tf_op jit(solution)/shard_map/all_to_all | solution.py:78
  203.2 9.3 %bitcast_convert_fusion = bf16[2,384,2,1024]{3,1,2,0:T(8,128)(2,1)} fusion(bf16[64,2,24,1024]{3,2,1,0:T(8,128)(2,1)} %bitcast.7, bf16[64,24,2,384]{3,1,2,0:T(8,128)(2,1)S(1)} %get-tuple-element.44), kind=kOutput, calls=%fused_computation.6 | convolution fusion | flops 4833411072 | bytes 11796480 | tf_op jit(solution)/shard_map/srlh,scrd->lhcd/dot_general | solution.py:122
  212.5 4.6 %copy.91 = bf16[2,384,2,1024]{1,3,2,0:T(8,128)(2,1)} copy(bf16[2,384,2,1024]{3,1,2,0:T(8,128)(2,1)} %bitcast_convert_fusion) | data formatting | bytes 6291456 | tf_op jit(solution)/shard_map/convert_element_type | solution.py:124
  217.1 4.8 %copy.93 = bf16[2,384,2048]{2,1,0:T(8,128)(2,1)} copy(bf16[2,384,2048]{1,2,0:T(8,128)(2,1)} %bitcast.217) | data formatting | bytes 6291456
  221.9 14.8 %multiply_convert_fusion.1 = (bf16[64,24,2,384]{3,1,2,0:T(8,128)(2,1)}, bf16[64,24,2,384]{3,1,2,0:T(8,128)(2,1)S(1)}) fusion(pred[24,2]{0,1:T(4,128)(4,1)S(1)} %iota_compare_fusion.4, f32[64,24,2,384,1]{3,1,4,2,0:T(8,128)} %copy-done.17, f32[64,24,2,384,1]{3,1,4,2,0:T(8,128)} %get-tuple-element.45, bf16[2,48,2,8,1024]{4,3,2,1,0:T(8,128)(2,1)} %bitcast.237, ...), kind=kOutput, calls=%fused_computation.29 | convolution fusion | flops 4850712576 | bytes 23593008 | tf_op jit(solution)/shard_map/scrd,lhcd->srlh/dot_general | solution.py:125
  238.2 6.5 %fusion.17 = bf16[2,2,1024,384]{2,3,1,0:T(8,128)(2,1)} fusion(bf16[64,2,24,1024]{3,2,1,0:T(8,128)(2,1)S(1)} %bitcast.228, bf16[64,24,2,384]{3,1,2,0:T(8,128)(2,1)S(1)} %get-tuple-element.43), kind=kOutput, calls=%fused_computation.37 | convolution fusion | flops 4833411072 | bytes 11796480 | tf_op jit(solution)/shard_map/scrd,srlh->lcdh/dot_general | solution.py:131
  244.6 5.0 %copy.85 = bf16[2,2,1024,384]{3,2,1,0:T(8,128)(2,1)} copy(bf16[2,2,1024,384]{2,3,1,0:T(8,128)(2,1)} %fusion.17) | data formatting | bytes 6291456 | tf_op jit(solution)/shard_map/convert_element_type | solution.py:133
  249.6 4.3 %fusion.39 = f32[64,24,1024,1]{2,1,3,0:T(8,128)S(1)} fusion(bf16[64,24,2,384]{3,1,2,0:T(8,128)(2,1)S(1)} %copy-done.15, bf16[2,2048,384]{2,1,0:T(8,128)(2,1)} %param.10), kind=kOutput, calls=%fused_computation.52 | convolution fusion | flops 2415919104 | bytes 10223616 | tf_op jit(solution)/shard_map/srlh,ldh->srd/dot_general | solution.py:139
  254.0 2.7 fusion.42
  256.7 3.1 fusion.16
  259.9 3.1 fusion.15
  263.6 3.3 copy.82
  266.9 15.1 %all-to-all-done.2 = bf16[128,24,1024]{2,1,0:T(8,128)(2,1)} async-done(((bf16[128,24,1024]{2,1,0:T(8,128)(2,1)}), bf16[128,24,1024]{2,1,0:T(8,128)(2,1)}, u32[]{:S(2)}, u32[]{:S(2)}) %all-to-all-start.2) | async-done | bytes 6291488 | tf_op jit(solution)/shard_map/all_to_all | solution.py:78
  282.0 10.1 %all-to-all-start.3 = ((bf16[128,24,1024]{2,1,0:T(8,128)(2,1)}), bf16[128,24,1024]{2,1,0:T(8,128)(2,1)}, u32[]{:S(2)}, u32[]{:S(2)}) async-start(bf16[128,24,1024]{2,1,0:T(8,128)(2,1)} %bitcast.214), calls=%async_computation.3 | async-start | bytes 12582912 | tf_op jit(solution)/shard_map/all_to_all | solution.py:78
  292.1 9.3 %fusion.18 = bf16[2,2,1024,384]{2,3,1,0:T(8,128)(2,1)} fusion(bf16[64,2,24,1024]{3,2,1,0:T(8,128)(2,1)} %bitcast.222, bf16[64,24,2,384]{3,1,2,0:T(8,128)(2,1)S(1)} %copy-done.13), kind=kOutput, calls=%fused_computation.38 | convolution fusion | flops 4833411072 | bytes 11796480 | tf_op jit(solution)/shard_map/scrd,srlh->lcdh/dot_general | solution.py:134
  301.4 4.7 %copy.88 = bf16[2,2,1024,384]{3,2,1,0:T(8,128)(2,1)} copy(bf16[2,2,1024,384]{2,3,1,0:T(8,128)(2,1)} %fusion.18) | data formatting | bytes 6291456 | tf_op jit(solution)/shard_map/convert_element_type | solution.py:136
  306.1 4.6 %fusion.61 = f32[3072,128]{1,0:T(8,128)S(1)} fusion(bf16[3072,1024]{1,0:T(8,128)(2,1)} %bitcast.30, bf16[128,1024]{1,0:T(8,128)(2,1)S(1)} %copy-done.6), kind=kOutput, calls=%fused_computation.89 | convolution fusion | flops 805306368 | bytes 8126464 | tf_op jit(solution)/shard_map/dot_general | solution.py:116
  313.1 4.7 %fusion.35 = f32[256,1024]{1,0:T(8,128)S(1)} fusion(bf16[3072,1024]{1,0:T(8,128)(2,1)} %bitcast.30, bf16[384,8,2,128]{3,2,1,0:T(2,128)(2,1)S(1)} %bitcast.216), kind=kOutput, calls=%fused_computation.48 | convolution fusion | flops 1610612736 | bytes 8912896 | tf_op jit(solution)/shard_map/dot_general | solution.py:110
  319.4 56.5 %psum.7 = f32[128,8]{1,0:T(8,128)S(1)} all-reduce(f32[128,8]{1,0:T(8,128)S(1)} %select_reduce_fusion.2), channel_id=1, replica_groups=mesh['dp'=64,'col'=2] {'col'}, use_global_device_ids=true, to_apply=%region_8.9 | all-reduce | flops 1024 | bytes 8192 | tf_op jit(solution)/shard_map/psum | solution.py:146
  376.7 4.6 %convolution_convert_fusion.1 = bf16[128,1024]{1,0:T(8,128)(2,1)} fusion(bf16[128,3072]{0,1:T(8,128)(2,1)S(1)} %bitcast.230, bf16[3072,1024]{1,0:T(8,128)(2,1)} %bitcast.58), kind=kOutput, calls=%fused_computation.65 | convolution fusion | flops 805437440 | bytes 7340032 | tf_op jit(solution)/shard_map/dot_general | solution.py:88
  (82 shorter events, 16.0 us)
Async XLA Ops:
  0.6 8.6 %copy-start = (bf16[128,2048]{1,0:T(8,128)(2,1)S(1)}, bf16[128,2048]{1,0:T(8,128)(2,1)}, u32[]{:S(2)}) copy-start(bf16[128,2048]{1,0:T(8,128)(2,1)} %param.7) | copy-start | bytes 1572868
  0.6 2.9 copy-start.7
  2.9 7.4 %copy-start.5 = (bf16[128,1024]{1,0:T(8,128)(2,1)S(1)}, bf16[128,1024]{1,0:T(8,128)(2,1)}, u32[]{:S(2)}) copy-start(bf16[128,1024]{1,0:T(8,128)(2,1)} %param.13) | copy-start | bytes 786436
  3.6 7.7 %copy-start.3 = (s32[128,8]{1,0:T(8,128)}, s32[128,8]{1,0:T(8,128)S(1)}, u32[]{:S(2)}) copy-start(s32[128,8]{1,0:T(8,128)S(1)} %copy.74) | copy-start | bytes 12292
  95.9 90.5 %all-to-all-start = ((bf16[128,24,1024]{2,1,0:T(8,128)(2,1)}), bf16[128,24,1024]{2,1,0:T(8,128)(2,1)}, u32[]{:S(2)}, u32[]{:S(2)}) async-start(bf16[128,24,1024]{2,1,0:T(8,128)(2,1)} %bitcast.212), calls=%async_computation | async-start | bytes 12582912 | tf_op jit(solution)/shard_map/all_to_all | solution.py:50
  108.9 2.0 copy-start.9
  109.1 9.5 %slice-start = ((s8[6291456]{0:T(1024)(128)(4,1)}), s8[4194304]{0:T(1024)(128)(4,1)S(1)}, s32[]{:S(2)}) async-start(s8[6291456]{0:T(1024)(128)(4,1)} %bitcast.223), calls=%async_computation.4 | async-start | bytes 8388608
  110.9 7.7 %slice-start.1 = ((s8[6291456]{0:T(1024)(128)(4,1)}), s8[2097152]{0:T(1024)(128)(4,1)S(1)}, s32[]{:S(2)}) async-start(s8[6291456]{0:T(1024)(128)(4,1)} %bitcast.223), calls=%async_computation.5 | async-start | bytes 4194304
  110.9 7.7 %copy-start.11 = (bf16[2,2048,384]{2,1,0:T(8,128)(2,1)S(1)}, bf16[2,2048,384]{2,1,0:T(8,128)(2,1)}, u32[]{:S(2)}) copy-start(bf16[2,2048,384]{2,1,0:T(8,128)(2,1)} %param.11) | copy-start | bytes 9437188
  118.6 7.5 %copy-start.17 = (f32[64,24,2,384,1]{3,1,4,2,0:T(8,128)}, f32[64,24,2,384,1]{3,1,4,2,0:T(8,128)S(1)}, u32[]{:S(2)}) copy-start(f32[64,24,2,384,1]{3,1,4,2,0:T(8,128)S(1)} %fusion.60) | copy-start | bytes 14155780
  118.7 7.4 %copy-start.8 = (bf16[2,384,2048]{2,1,0:T(8,128)(2,1)S(1)}, bf16[2,384,2048]{2,1,0:T(8,128)(2,1)}, u32[]{:S(2)}) copy-start(bf16[2,384,2048]{2,1,0:T(8,128)(2,1)} %param.12) | copy-start | bytes 9437188
  193.2 88.8 %all-to-all-start.2 = ((bf16[128,24,1024]{2,1,0:T(8,128)(2,1)}), bf16[128,24,1024]{2,1,0:T(8,128)(2,1)}, u32[]{:S(2)}, u32[]{:S(2)}) async-start(bf16[128,24,1024]{2,1,0:T(8,128)(2,1)} %bitcast.213), calls=%async_computation.2 | async-start | bytes 12582912 | tf_op jit(solution)/shard_map/all_to_all | solution.py:78
  217.1 21.0 %slice-start.2 = ((s8[6291456]{0:T(1024)(128)(4,1)}), s8[2097152]{0:T(1024)(128)(4,1)S(1)}, s32[]{:S(2)}) async-start(s8[6291456]{0:T(1024)(128)(4,1)} %bitcast.226), calls=%async_computation.6 | async-start | bytes 4194304
  221.9 16.2 %slice-start.3 = ((s8[6291456]{0:T(1024)(128)(4,1)}), s8[4194304]{0:T(1024)(128)(4,1)S(1)}, s32[]{:S(2)}) async-start(s8[6291456]{0:T(1024)(128)(4,1)} %bitcast.226), calls=%async_computation.7 | async-start | bytes 8388608
  236.8 1.4 copy-start.14
  244.6 5.0 %copy-start.15 = (bf16[64,24,2,384]{3,1,2,0:T(8,128)(2,1)S(1)}, bf16[64,24,2,384]{3,1,2,0:T(8,128)(2,1)}, u32[]{:S(2)}) copy-start(bf16[64,24,2,384]{3,1,2,0:T(8,128)(2,1)} %copy-done.14) | copy-start | bytes 7077892
  249.6 4.3 %copy-start.10 = (bf16[2,2048,384]{2,1,0:T(8,128)(2,1)S(1)}, bf16[2,2048,384]{2,1,0:T(8,128)(2,1)}, u32[]{:S(2)}) copy-start(bf16[2,2048,384]{2,1,0:T(8,128)(2,1)} %param.10) | copy-start | bytes 9437188
  249.6 4.3 %copy-start.16 = (bf16[64,24,2,384]{3,1,2,0:T(8,128)(2,1)S(1)}, bf16[64,24,2,384]{3,1,2,0:T(8,128)(2,1)}, u32[]{:S(2)}) copy-start(bf16[64,24,2,384]{3,1,2,0:T(8,128)(2,1)} %copy-done.14) | copy-start | bytes 7077892
  253.9 2.8 copy-start.12
  253.9 2.7 copy-start.13
  282.0 94.6 %all-to-all-start.3 = ((bf16[128,24,1024]{2,1,0:T(8,128)(2,1)}), bf16[128,24,1024]{2,1,0:T(8,128)(2,1)}, u32[]{:S(2)}, u32[]{:S(2)}) async-start(bf16[128,24,1024]{2,1,0:T(8,128)(2,1)} %bitcast.214), calls=%async_computation.3 | async-start | bytes 12582912 | tf_op jit(solution)/shard_map/all_to_all | solution.py:78
  301.4 4.7 %copy-start.6 = (bf16[128,1024]{1,0:T(8,128)(2,1)S(1)}, bf16[128,1024]{1,0:T(8,128)(2,1)}, u32[]{:S(2)}) copy-start(bf16[128,1024]{1,0:T(8,128)(2,1)} %param.13) | copy-start | bytes 786436
  313.0 5.5 %copy-start.4 = (s32[128,8]{1,0:T(8,128)S(1)}, s32[128,8]{1,0:T(8,128)}, u32[]{:S(2)}) copy-start(s32[128,8]{1,0:T(8,128)} %copy-done.3) | copy-start | bytes 12292
  313.1 63.5 %copy-start.2 = (bf16[128,1536]{0,1:T(8,128)(2,1)S(1)}, bf16[128,1536]{0,1:T(8,128)(2,1)}, u32[]{:S(2)}) copy-start(bf16[128,1536]{0,1:T(8,128)(2,1)} %copy.80) | copy-start | bytes 1179652
  376.7 4.6 %copy-start.1 = (bf16[128,2048]{1,0:T(8,128)(2,1)S(1)}, bf16[128,2048]{1,0:T(8,128)(2,1)}, u32[]{:S(2)}) copy-start(bf16[128,2048]{1,0:T(8,128)(2,1)} %param.7) | copy-start | bytes 1572868

commit v2 on v1

--- a/solution.py
+++ b/solution.py
@@ -73,8 +73,10 @@
             (tok_count, owners, cols, rows_per_owner),
         )
 
-    def send_back(halves):
-        part = jnp.stack([h.astype(jnp.bfloat16) for h in halves], axis=1)
+    def pack(halves):
+        return jnp.stack([h.astype(jnp.bfloat16) for h in halves], axis=1)
+
+    def send_back(part):
         got = lax.all_to_all(
             part.reshape(owners * cols, rows_per_owner, half_width), both, 0, 0, tiled=True
         )
@@ -101,8 +103,9 @@
         jnp.einsum("srlh,lhd->srd", hidden, w, preferred_element_type=jnp.float32)
         for w in halves_of(w_down, 2)
     ]
-    d_out, out_halves = lax.optimization_barrier((d_out, out_halves))
-    got_out = send_back(out_halves)
+    out_part = pack(out_halves)
+    d_out, out_part = lax.optimization_barrier((d_out, out_part))
+    got_out = send_back(out_part)
     stacked = jnp.broadcast_to(
         jnp.stack([weight_hi, weight_lo]).reshape(2, tok_count, owners, 1, rows_per_owner),
         (2, tok_count, owners, cols, rows_per_owner),
@@ -134,13 +137,13 @@
     grad_up = jnp.einsum(
         "scrd,srlh->lcdh", row_block, d_up, preferred_element_type=jnp.float32
     ).astype(jnp.bfloat16).reshape(w_up.shape)
-    got_grad = send_back(
+    got_grad = send_back(pack(
         [
             jnp.einsum("srlh,ldh->srd", d_gate, wg, preferred_element_type=jnp.float32)
             + jnp.einsum("srlh,ldh->srd", d_up, wu, preferred_element_type=jnp.float32)
             for wg, wu in zip(halves_of(w_gate, 1), halves_of(w_up, 1))
         ]
-    )
+    ))
     grad_tokens = combine(picker, got_grad).astype(jnp.bfloat16)
     prob_part, mixed = lax.optimization_barrier((prob_part, mixed))
     grad_probs = lax.psum(prob_part, "col")

time: 389 us -> 400 us (1.028)
  blocking collectives: 137 us -> 51.8 us
  waiting for transfers between devices: 67.5 us -> 147 us
  starting transfers between devices: 31.8 us -> 40.4 us
  matrix products: 92.1 us -> 97.1 us
    all_to_all x1 -> x0, blocking collectives: 80.2 us -> none  [dispatch(): got = lax.all_to_all(sent, both, 0, 0, tiled=True)]
    all_to_all x1 -> x2, waiting for transfers between devices: 52.4 us -> 125 us  [dispatch(): got = lax.all_to_all(sent, both, 0, 0, tiled=True)]
    all_to_all x1 -> x2, starting transfers between devices: 11.7 us -> 20.3 us  [dispatch(): got = lax.all_to_all(sent, both, 0, 0, tiled=True)]
    optimization_barrier x0 -> x1, local copies, waits for them, and re-layouts: none -> 6.54 us  [body(): d_out, out_part = lax.optimization_barrier((d_out, out_part))]
    all_to_all x2, waiting for transfers between devices: 15.1 us -> 21.5 us  [send_back(): lax.all_to_all(part.reshape(owners * cols, rows_per_owner, half_width), b...]
    dot_general x1, matrix products: 7.4 us -> 13.7 us  [body(): jnp.einsum('scrd,lcdh->srlh', row_block, w_up_h, preferred_element_type=j...]
    psum x1, blocking collectives: 56.5 us -> 51.8 us  [body(): grad_probs = lax.psum(prob_part, 'col')]
    unnamed x48 -> x36, local copies, waits for them, and re-layouts: 8.57 us -> 6.37 us
  transfers between devices with their start and end apart: 3 -> 4, of which waited for: 2 -> 3; matrix products, arithmetic and copies ran while one was open for 30% -> 32% of each run, Pallas kernels for 0% -> 0%
where the time goes in v2:
time: 400 us; the launch traced here: 392 us
  waiting for transfers between devices  147 us (37%)
  matrix products  97.1 us (24%)
  blocking collectives  51.8 us (13%)
  local copies, waits for them, and re-layouts  42.8 us (11%)
  starting transfers between devices  40.4 us (10%)
  other arithmetic  12 us (3%)
    all_to_all x2, waiting for transfers between devices, dispatch(): got = lax.all_to_all(sent, both, 0, 0, tiled=True)  125 us
    psum x1, blocking collectives, body(): grad_probs = lax.psum(prob_part, 'col')  51.8 us
    all_to_all x2, waiting for transfers between devices, send_back(): lax.all_to_all(part.reshape(owners * cols, rows_per_owner, half_width), b...  21.5 us
    all_to_all x2, starting transfers between devices, dispatch(): got = lax.all_to_all(sent, both, 0, 0, tiled=True)  20.3 us
    all_to_all x2, starting transfers between devices, send_back(): lax.all_to_all(part.reshape(owners * cols, rows_per_owner, half_width), b...  20.1 us
    dot_general x1, matrix products, body(): jnp.einsum('scrd,lhcd->srlh', d_out, w_down_h, preferred_element_type=jnp...  13.8 us
    dot_general x1, matrix products, body(): jnp.einsum('scrd,lcdh->srlh', row_block, w_up_h, preferred_element_type=j...  13.7 us
    dot_general x1, matrix products, body(): jnp.einsum('scrd,srlh->lcdh', row_block, d_gate, preferred_element_type=j...  9.45 us
  transfers between devices with their start and end apart: 4, of which 3 were waited for; matrix products, arithmetic and copies ran while one was open for 32% of the time, Pallas kernels for 0%

profile of v2, /device:TPU:82, one launch (start us, length us, event | category | flops | bytes accessed | tf_op | source)
XLA Modules:
  0.0 392.4 jit_solution(17027068105571947007)
XLA Ops:
  2.9 3.1 fusion.11
  10.7 3.5 broadcast_in_dim.82
  14.2 3.4 broadcast_in_dim.86
  17.6 10.3 %all-to-all-start.1 = ((bf16[128,24,1024]{2,1,0:T(8,128)(2,1)}), bf16[128,24,1024]{2,1,0:T(8,128)(2,1)}, u32[]{:S(2)}, u32[]{:S(2)}) async-start(bf16[128,24,1024]{2,1,0:T(8,128)(2,1)} %bitcast.217), calls=%async_computation.1 | async-start | bytes 12582912 | tf_op jit(solution)/shard_map/all_to_all | solution.py:50
  28.2 80.6 %all-to-all-done.1 = bf16[128,24,1024]{2,1,0:T(8,128)(2,1)} async-done(((bf16[128,24,1024]{2,1,0:T(8,128)(2,1)}), bf16[128,24,1024]{2,1,0:T(8,128)(2,1)}, u32[]{:S(2)}, u32[]{:S(2)}) %all-to-all-start.1) | async-done | bytes 6291488 | tf_op jit(solution)/shard_map/all_to_all | solution.py:50
  108.8 10.0 %all-to-all-start = ((bf16[128,24,1024]{2,1,0:T(8,128)(2,1)}), bf16[128,24,1024]{2,1,0:T(8,128)(2,1)}, u32[]{:S(2)}, u32[]{:S(2)}) async-start(bf16[128,24,1024]{2,1,0:T(8,128)(2,1)} %bitcast.214), calls=%async_computation | async-start | bytes 12582912 | tf_op jit(solution)/shard_map/all_to_all | solution.py:50
  121.7 8.3 %fusion.62 = f32[64,24,2,384,1]{3,1,4,2,0:T(8,128)S(1)} fusion(bf16[64,2,24,1024,1]{3,2,1,4,0:T(8,128)(2,1)} %bitcast.10, bf16[2,2,1024,384,1]{3,2,1,0,4:T(8,128)(2,1)} %bitcast.230), kind=kOutput, calls=%fused_computation.88 | convolution fusion | flops 4831838208 | bytes 14155776 | tf_op jit(solution)/shard_map/scrd,lcdh->srlh/dot_general | solution.py:95
  130.0 13.7 %multiply_convert_fusion.3 = (bf16[64,24,2,384]{3,1,2,0:T(8,128)(2,1)S(1)}, f32[64,24,2,384,1]{3,1,4,2,0:T(8,128)}) fusion(pred[24,2]{0,1:T(4,128)(4,1)S(1)} %iota_compare_fusion.4, f32[64,24,2,384,1]{3,1,4,2,0:T(8,128)S(1)} %fusion.62, bf16[64,2,24,1024,1]{3,2,1,4,0:T(8,128)(2,1)} %bitcast.10, bf16[2,2,1024,384,1]{3,2,1,0,4:T(8,128)(2,1)S(1)} %bitcast.231), kind=kOutput, calls=%fused_computation.33 | convolution fusion | flops 4841275392 | bytes 21233712 | tf_op jit(solution)/shard_map/scrd,lcdh->srlh/dot_general | solution.py:96
  143.7 2.9 fusion.16
  146.6 2.9 fusion.15
  149.5 3.1 pad_maximum_fusion
  152.7 44.9 %all-to-all-done = bf16[128,24,1024]{2,1,0:T(8,128)(2,1)} async-done(((bf16[128,24,1024]{2,1,0:T(8,128)(2,1)}), bf16[128,24,1024]{2,1,0:T(8,128)(2,1)}, u32[]{:S(2)}, u32[]{:S(2)}) %all-to-all-start) | async-done | bytes 6291488 | tf_op jit(solution)/shard_map/all_to_all | solution.py:50
  197.6 6.5 %copy.76 = bf16[64,2,24,1024]{3,2,1,0:T(8,128)(2,1)} copy(bf16[64,2,24,1024]{3,2,0,1:T(8,128)(2,1)} %pad_maximum_fusion) | data formatting | bytes 12582912 | tf_op jit(solution)/shard_map/optimization_barrier | solution.py:107
  204.1 10.1 %all-to-all-start.2 = ((bf16[128,24,1024]{2,1,0:T(8,128)(2,1)}), bf16[128,24,1024]{2,1,0:T(8,128)(2,1)}, u32[]{:S(2)}, u32[]{:S(2)}) async-start(bf16[128,24,1024]{2,1,0:T(8,128)(2,1)} %bitcast.216), calls=%async_computation.2 | async-start | bytes 12582912 | tf_op jit(solution)/shard_map/all_to_all | solution.py:80
  214.2 13.8 %multiply_convert_fusion.1 = (bf16[64,24,2,384]{3,1,2,0:T(8,128)(2,1)S(1)}, bf16[64,24,2,384]{3,1,2,0:T(8,128)(2,1)S(1)}) fusion(pred[24,2]{0,1:T(4,128)(4,1)S(1)} %iota_compare_fusion.4, f32[64,24,2,384,1]{3,1,4,2,0:T(8,128)} %copy-done.15, f32[64,24,2,384,1]{3,1,4,2,0:T(8,128)} %get-tuple-element.43, bf16[2,48,2,8,1024]{4,3,2,1,0:T(8,128)(2,1)} %bitcast.229, ...), kind=kOutput, calls=%fused_computation.31 | convolution fusion | flops 4850712576 | bytes 23593008 | tf_op jit(solution)/shard_map/scrd,lhcd->srlh/dot_general | solution.py:128
  228.0 2.7 fusion.41
  230.6 9.4 %fusion.19 = bf16[2,2,1024,384]{2,3,1,0:T(8,128)(2,1)} fusion(bf16[64,2,24,1024]{3,2,1,0:T(8,128)(2,1)} %bitcast.8, bf16[64,24,2,384]{3,1,2,0:T(8,128)(2,1)S(1)} %get-tuple-element.41), kind=kOutput, calls=%fused_computation.41 | convolution fusion | flops 4833411072 | bytes 11796480 | tf_op jit(solution)/shard_map/scrd,srlh->lcdh/dot_general | solution.py:134
  240.1 3.3 fusion.18
  246.1 2.9 fusion.17
  249.6 3.3 copy.82
  252.9 4.6 %copy.85 = bf16[2,2,1024,384]{3,2,1,0:T(8,128)(2,1)} copy(bf16[2,2,1024,384]{2,3,1,0:T(8,128)(2,1)} %fusion.19) | data formatting | bytes 6291456 | tf_op jit(solution)/shard_map/convert_element_type | solution.py:136
  257.5 9.3 %fusion.20 = bf16[2,2,1024,384]{2,3,1,0:T(8,128)(2,1)} fusion(bf16[64,2,24,1024]{3,2,1,0:T(8,128)(2,1)} %bitcast.8, bf16[64,24,2,384]{3,1,2,0:T(8,128)(2,1)S(1)} %get-tuple-element.40), kind=kOutput, calls=%fused_computation.42 | convolution fusion | flops 4833411072 | bytes 11796480 | tf_op jit(solution)/shard_map/scrd,srlh->lcdh/dot_general | solution.py:137
  266.8 4.6 %copy.88 = bf16[2,2,1024,384]{3,2,1,0:T(8,128)(2,1)} copy(bf16[2,2,1024,384]{2,3,1,0:T(8,128)(2,1)} %fusion.20) | data formatting | bytes 6291456 | tf_op jit(solution)/shard_map/convert_element_type | solution.py:139
  271.4 21.5 %all-to-all-done.2 = bf16[128,24,1024]{2,1,0:T(8,128)(2,1)} async-done(((bf16[128,24,1024]{2,1,0:T(8,128)(2,1)}), bf16[128,24,1024]{2,1,0:T(8,128)(2,1)}, u32[]{:S(2)}, u32[]{:S(2)}) %all-to-all-start.2) | async-done | bytes 6291488 | tf_op jit(solution)/shard_map/all_to_all | solution.py:80
  292.9 10.0 %all-to-all-start.3 = ((bf16[128,24,1024]{2,1,0:T(8,128)(2,1)}), bf16[128,24,1024]{2,1,0:T(8,128)(2,1)}, u32[]{:S(2)}, u32[]{:S(2)}) async-start(bf16[128,24,1024]{2,1,0:T(8,128)(2,1)} %bitcast.215), calls=%async_computation.3 | async-start | bytes 12582912 | tf_op jit(solution)/shard_map/all_to_all | solution.py:80
  303.0 9.3 %bitcast_convert_fusion = bf16[2,384,2,1024]{3,1,2,0:T(8,128)(2,1)} fusion(bf16[64,2,24,1024]{3,2,1,0:T(8,128)(2,1)} %bitcast.7, bf16[64,24,2,384]{3,1,2,0:T(8,128)(2,1)S(1)} %copy-done.14), kind=kOutput, calls=%fused_computation.6 | convolution fusion | flops 4833411072 | bytes 11796480 | tf_op jit(solution)/shard_map/srlh,scrd->lhcd/dot_general | solution.py:125
  312.3 4.6 %copy.91 = bf16[2,384,2,1024]{1,3,2,0:T(8,128)(2,1)} copy(bf16[2,384,2,1024]{3,1,2,0:T(8,128)(2,1)} %bitcast_convert_fusion) | data formatting | bytes 6291456 | tf_op jit(solution)/shard_map/convert_element_type | solution.py:127
  316.9 4.7 %copy.93 = bf16[2,384,2048]{2,1,0:T(8,128)(2,1)} copy(bf16[2,384,2048]{1,2,0:T(8,128)(2,1)} %bitcast.219) | data formatting | bytes 6291456
  321.6 4.6 %fusion.63 = f32[3072,128]{1,0:T(8,128)S(1)} fusion(bf16[3072,1024]{1,0:T(8,128)(2,1)} %bitcast.30, bf16[128,1024]{1,0:T(8,128)(2,1)S(1)} %copy-done.6), kind=kOutput, calls=%fused_computation.89 | convolution fusion | flops 805306368 | bytes 8126464 | tf_op jit(solution)/shard_map/dot_general | solution.py:119
  328.6 4.7 %fusion.37 = f32[256,1024]{1,0:T(8,128)S(1)} fusion(bf16[3072,1024]{1,0:T(8,128)(2,1)} %bitcast.30, bf16[384,8,2,128]{3,2,1,0:T(2,128)(2,1)S(1)} %bitcast.218), kind=kOutput, calls=%fused_computation.48 | convolution fusion | flops 1610612736 | bytes 8912896 | tf_op jit(solution)/shard_map/dot_general | solution.py:113
  334.9 51.8 %psum.7 = f32[128,8]{1,0:T(8,128)S(1)} all-reduce(f32[128,8]{1,0:T(8,128)S(1)} %select_reduce_fusion.2), channel_id=1, replica_groups=mesh['dp'=64,'col'=2] {'col'}, use_global_device_ids=true, to_apply=%region_8.9 | all-reduce | flops 1024 | bytes 8192 | tf_op jit(solution)/shard_map/psum | solution.py:149
  387.6 4.6 %convolution_convert_fusion.1 = bf16[128,1024]{1,0:T(8,128)(2,1)} fusion(bf16[128,3072]{0,1:T(8,128)(2,1)S(1)} %bitcast.224, bf16[3072,1024]{1,0:T(8,128)(2,1)} %bitcast.58), kind=kOutput, calls=%fused_computation.65 | convolution fusion | flops 805437440 | bytes 7340032 | tf_op jit(solution)/shard_map/dot_general | solution.py:90
  (69 shorter events, 18.0 us)
Async XLA Ops:
  0.6 8.0 %copy-start = (bf16[128,2048]{1,0:T(8,128)(2,1)S(1)}, bf16[128,2048]{1,0:T(8,128)(2,1)}, u32[]{:S(2)}) copy-start(bf16[128,2048]{1,0:T(8,128)(2,1)} %param.7) | copy-start | bytes 1572868
  0.6 2.1 copy-start.7
  0.7 5.4 %copy-start.8 = (f32[128,8]{0,1:T(8,128)S(1)}, f32[128,8]{0,1:T(8,128)}, u32[]{:S(2)}) copy-start(f32[128,8]{0,1:T(8,128)} %param.9) | copy-start | bytes 12292
  2.1 7.5 %copy-start.5 = (bf16[128,1024]{1,0:T(8,128)(2,1)S(1)}, bf16[128,1024]{1,0:T(8,128)(2,1)}, u32[]{:S(2)}) copy-start(bf16[128,1024]{1,0:T(8,128)(2,1)} %param.13) | copy-start | bytes 786436
  2.9 7.8 %copy-start.3 = (s32[128,8]{1,0:T(8,128)}, s32[128,8]{1,0:T(8,128)S(1)}, u32[]{:S(2)}) copy-start(s32[128,8]{1,0:T(8,128)S(1)} %copy.74) | copy-start | bytes 12292
  17.6 91.2 %all-to-all-start.1 = ((bf16[128,24,1024]{2,1,0:T(8,128)(2,1)}), bf16[128,24,1024]{2,1,0:T(8,128)(2,1)}, u32[]{:S(2)}, u32[]{:S(2)}) async-start(bf16[128,24,1024]{2,1,0:T(8,128)(2,1)} %bitcast.217), calls=%async_computation.1 | async-start | bytes 12582912 | tf_op jit(solution)/shard_map/all_to_all | solution.py:50
  108.8 88.8 %all-to-all-start = ((bf16[128,24,1024]{2,1,0:T(8,128)(2,1)}), bf16[128,24,1024]{2,1,0:T(8,128)(2,1)}, u32[]{:S(2)}, u32[]{:S(2)}) async-start(bf16[128,24,1024]{2,1,0:T(8,128)(2,1)} %bitcast.214), calls=%async_computation | async-start | bytes 12582912 | tf_op jit(solution)/shard_map/all_to_all | solution.py:50
  121.7 8.3 %copy-start.11 = (bf16[2,2048,384]{2,1,0:T(8,128)(2,1)S(1)}, bf16[2,2048,384]{2,1,0:T(8,128)(2,1)}, u32[]{:S(2)}) copy-start(bf16[2,2048,384]{2,1,0:T(8,128)(2,1)} %param.11) | copy-start | bytes 9437188
  130.0 13.8 %copy-start.15 = (f32[64,24,2,384,1]{3,1,4,2,0:T(8,128)}, f32[64,24,2,384,1]{3,1,4,2,0:T(8,128)S(1)}, u32[]{:S(2)}) copy-start(f32[64,24,2,384,1]{3,1,4,2,0:T(8,128)S(1)} %fusion.62) | copy-start | bytes 14155780
  130.0 13.7 %copy-start.9 = (bf16[2,384,2048]{2,1,0:T(8,128)(2,1)S(1)}, bf16[2,384,2048]{2,1,0:T(8,128)(2,1)}, u32[]{:S(2)}) copy-start(bf16[2,384,2048]{2,1,0:T(8,128)(2,1)} %param.12) | copy-start | bytes 9437188
  143.7 2.9 copy-start.13
  204.1 88.8 %all-to-all-start.2 = ((bf16[128,24,1024]{2,1,0:T(8,128)(2,1)}), bf16[128,24,1024]{2,1,0:T(8,128)(2,1)}, u32[]{:S(2)}, u32[]{:S(2)}) async-start(bf16[128,24,1024]{2,1,0:T(8,128)(2,1)} %bitcast.216), calls=%async_computation.2 | async-start | bytes 12582912 | tf_op jit(solution)/shard_map/all_to_all | solution.py:80
  214.2 13.8 %copy-start.10 = (bf16[2,2048,384]{2,1,0:T(8,128)(2,1)S(1)}, bf16[2,2048,384]{2,1,0:T(8,128)(2,1)}, u32[]{:S(2)}) copy-start(bf16[2,2048,384]{2,1,0:T(8,128)(2,1)} %param.10) | copy-start | bytes 9437188
  230.6 9.5 %copy-start.12 = (bf16[2,2048,384]{2,1,0:T(8,128)(2,1)S(1)}, bf16[2,2048,384]{2,1,0:T(8,128)(2,1)}, u32[]{:S(2)}) copy-start(bf16[2,2048,384]{2,1,0:T(8,128)(2,1)} %param.11) | copy-start | bytes 9437188
  292.9 10.0 %copy-start.14 = (bf16[64,24,2,384]{3,1,2,0:T(8,128)(2,1)S(1)}, bf16[64,24,2,384]{3,1,2,0:T(8,128)(2,1)}, u32[]{:S(2)}) copy-start(bf16[64,24,2,384]{3,1,2,0:T(8,128)(2,1)} %copy-done.13) | copy-start | bytes 7077892
  292.9 94.5 %all-to-all-start.3 = ((bf16[128,24,1024]{2,1,0:T(8,128)(2,1)}), bf16[128,24,1024]{2,1,0:T(8,128)(2,1)}, u32[]{:S(2)}, u32[]{:S(2)}) async-start(bf16[128,24,1024]{2,1,0:T(8,128)(2,1)} %bitcast.215), calls=%async_computation.3 | async-start | bytes 12582912 | tf_op jit(solution)/shard_map/all_to_all | solution.py:80
  316.9 4.7 %copy-start.6 = (bf16[128,1024]{1,0:T(8,128)(2,1)S(1)}, bf16[128,1024]{1,0:T(8,128)(2,1)}, u32[]{:S(2)}) copy-start(bf16[128,1024]{1,0:T(8,128)(2,1)} %param.13) | copy-start | bytes 786436
  328.6 5.5 %copy-start.4 = (s32[128,8]{1,0:T(8,128)S(1)}, s32[128,8]{1,0:T(8,128)}, u32[]{:S(2)}) copy-start(s32[128,8]{1,0:T(8,128)} %copy-done.3) | copy-start | bytes 12292
  328.6 58.9 %copy-start.2 = (bf16[128,1536]{0,1:T(8,128)(2,1)S(1)}, bf16[128,1536]{0,1:T(8,128)(2,1)}, u32[]{:S(2)}) copy-start(bf16[128,1536]{0,1:T(8,128)(2,1)} %copy.80) | copy-start | bytes 1179652
  387.6 4.6 %copy-start.1 = (bf16[128,2048]{1,0:T(8,128)(2,1)S(1)}, bf16[128,2048]{1,0:T(8,128)(2,1)}, u32[]{:S(2)}) copy-start(bf16[128,2048]{1,0:T(8,128)(2,1)} %param.7) | copy-start | bytes 1572868

commit v3 on v1

--- a/solution.py
+++ b/solution.py
@@ -73,8 +73,8 @@
             (tok_count, owners, cols, rows_per_owner),
         )
 
-    def send_back(halves):
-        part = jnp.stack([h.astype(jnp.bfloat16) for h in halves], axis=1)
+    def send_back(part):
+        part = part.astype(jnp.bfloat16)
         got = lax.all_to_all(
             part.reshape(owners * cols, rows_per_owner, half_width), both, 0, 0, tiled=True
         )
@@ -97,10 +97,7 @@
     sigmoid_g = jax.nn.sigmoid(gate_acts)
     silu_g = gate_acts * sigmoid_g
     hidden = (silu_g * up_acts).astype(jnp.bfloat16)
-    out_halves = [
-        jnp.einsum("srlh,lhd->srd", hidden, w, preferred_element_type=jnp.float32)
-        for w in halves_of(w_down, 2)
-    ]
+    out_halves = jnp.einsum("srlh,lhjd->sjrd", hidden, w_down_h, preferred_element_type=jnp.float32)
     d_out, out_halves = lax.optimization_barrier((d_out, out_halves))
     got_out = send_back(out_halves)
     stacked = jnp.broadcast_to(
@@ -135,11 +132,8 @@
         "scrd,srlh->lcdh", row_block, d_up, preferred_element_type=jnp.float32
     ).astype(jnp.bfloat16).reshape(w_up.shape)
     got_grad = send_back(
-        [
-            jnp.einsum("srlh,ldh->srd", d_gate, wg, preferred_element_type=jnp.float32)
-            + jnp.einsum("srlh,ldh->srd", d_up, wu, preferred_element_type=jnp.float32)
-            for wg, wu in zip(halves_of(w_gate, 1), halves_of(w_up, 1))
-        ]
+        jnp.einsum("srlh,ljdh->sjrd", d_gate, w_gate_h, preferred_element_type=jnp.float32)
+        + jnp.einsum("srlh,ljdh->sjrd", d_up, w_up_h, preferred_element_type=jnp.float32)
     )
     grad_tokens = combine(picker, got_grad).astype(jnp.bfloat16)
     prob_part, mixed = lax.optimization_barrier((prob_part, mixed))

time: 389 us -> 404 us (1.039)
  waiting for transfers between devices: 67.5 us -> 96.3 us
  local copies, waits for them, and re-layouts: 39.7 us -> 31.1 us
    all_to_all x2, waiting for transfers between devices: 15.1 us -> 42.9 us  [send_back(): lax.all_to_all(part.reshape(owners * cols, rows_per_owner, half_width), b...]
    another operation x5 -> x3, local copies, waits for them, and re-layouts: 6.73 us -> 0.11 us  [the longest x2 6.62 us: send_back(): part = jnp.stack([h.astype(jnp.bfloat16) for h in halves], axis=1)]
    dot_general x1, matrix products: 14.8 us -> 9.95 us  [body(): jnp.einsum('scrd,lhcd->srlh', d_out, w_down_h, preferred_element_type=jnp...]
    unnamed x48 -> x42, local copies, waits for them, and re-layouts: 8.57 us -> 7.03 us
    dot_general x6 -> x3, matrix products: 21.2 us -> 21.8 us  [the longest x1 7.53 us: body(): jnp.einsum('srlh,ljdh->sjrd', d_up, w_up_h, preferred_element_type=jnp.fl...]
  transfers between devices with their start and end apart: 3 -> 3, of which waited for: 2 -> 2; matrix products, arithmetic and copies ran while one was open for 30% -> 23% of each run, Pallas kernels for 0% -> 0%
where the time goes in v3:
time: 404 us; the launch traced here: 396 us
  blocking collectives  137 us (34%)
  waiting for transfers between devices  96.3 us (24%)
  matrix products  90.7 us (22%)
  starting transfers between devices  31.5 us (8%)
  local copies, waits for them, and re-layouts  31.1 us (8%)
  other arithmetic  9.01 us (2%)
    all_to_all x1, blocking collectives, dispatch(): got = lax.all_to_all(sent, both, 0, 0, tiled=True)  80.2 us
    psum x1, blocking collectives, body(): grad_probs = lax.psum(prob_part, 'col')  56.5 us
    all_to_all x1, waiting for transfers between devices, dispatch(): got = lax.all_to_all(sent, both, 0, 0, tiled=True)  53.4 us
    all_to_all x2, waiting for transfers between devices, send_back(): lax.all_to_all(part.reshape(owners * cols, rows_per_owner, half_width), b...  42.9 us
    all_to_all x2, starting transfers between devices, send_back(): lax.all_to_all(part.reshape(owners * cols, rows_per_owner, half_width), b...  19.7 us
    all_to_all x1, starting transfers between devices, dispatch(): got = lax.all_to_all(sent, both, 0, 0, tiled=True)  11.7 us
    dot_general x1, matrix products, body(): jnp.einsum('scrd,lhcd->srlh', d_out, w_down_h, preferred_element_type=jnp...  9.95 us
    dot_general x1, matrix products, body(): jnp.einsum('srlh,scrd->lhcd', hidden, d_out, preferred_element_type=jnp.f...  9.42 us
  transfers between devices with their start and end apart: 3, of which 2 were waited for; matrix products, arithmetic and copies ran while one was open for 23% of the time, Pallas kernels for 0%

profile of v3, /device:TPU:82, one launch (start us, length us, event | category | flops | bytes accessed | tf_op | source)
XLA Modules:
  0.0 396.5 jit_solution(10978684076308002926)
XLA Ops:
  4.3 3.1 fusion.10
  7.5 2.5 select_reduce_fusion
  10.0 1.0 convolution_convert_fusion
  11.0 1.0 multiply_convert_fusion
  12.1 3.4 broadcast_in_dim.86
  15.4 0.9 broadcast_in_dim.82
  16.4 80.2 %all_to_all.20 = bf16[128,24,1024]{2,1,0:T(8,128)(2,1)} all-to-all(bf16[128,24,1024]{2,1,0:T(8,128)(2,1)S(1)} %bitcast.192), channel_id=1, replica_groups=mesh['dp'=64,'col'=2] {'dp','col'}, dimensions={0} | all-to-all | bytes 12582912 | tf_op jit(solution)/shard_map/all_to_all | solution.py:50
  96.6 11.7 %all-to-all-start = ((bf16[128,24,1024]{2,1,0:T(8,128)(2,1)}), bf16[128,24,1024]{2,1,0:T(8,128)(2,1)}, u32[]{:S(2)}, u32[]{:S(2)}) async-start(bf16[128,24,1024]{2,1,0:T(8,128)(2,1)} %bitcast.191), calls=%async_computation | async-start | bytes 12582912 | tf_op jit(solution)/shard_map/all_to_all | solution.py:50
  108.3 0.9 copy.85
  109.7 1.7 copy.84
  111.5 7.7 %fusion.52 = f32[64,24,2,384,1]{3,1,4,2,0:T(8,128)S(1)} fusion(bf16[64,2,24,1024,1]{3,2,1,4,0:T(8,128)(2,1)} %bitcast.198, bf16[2,2,1024,384,1]{3,2,1,0,4:T(8,128)(2,1)S(1)} %bitcast.215), kind=kOutput, calls=%fused_computation.75 | convolution fusion | flops 4831838208 | bytes 14155776 | tf_op jit(solution)/shard_map/scrd,lcdh->srlh/dot_general | solution.py:93
  119.3 7.4 %multiply_convert_fusion.3 = (bf16[64,24,2,384]{3,1,2,0:T(8,128)(2,1)S(1)}, f32[64,24,2,384,1]{3,1,4,2,0:T(8,128)}) fusion(pred[24,2]{0,1:T(4,128)(4,1)S(1)} %iota_compare_fusion.4, f32[64,24,2,384,1]{3,1,4,2,0:T(8,128)S(1)} %fusion.52, bf16[64,2,24,1024,1]{3,2,1,4,0:T(8,128)(2,1)S(1)} %bitcast.203, bf16[2,2,1024,384,1]{3,2,1,0,4:T(8,128)(2,1)S(1)} %bitcast.216), kind=kOutput, calls=%fused_computation.27 | convolution fusion | flops 4841275392 | bytes 21233712 | tf_op jit(solution)/shard_map/scrd,lcdh->srlh/dot_general | solution.py:94
  126.6 7.0 %convolution_bitcast_fusion = bf16[64,2,24,1024]{3,2,1,0:T(8,128)(2,1)} fusion(bf16[2,48,2,8,1024]{4,3,2,1,0:T(8,128)(2,1)S(1)} %bitcast.212, bf16[64,24,2,384]{3,1,2,0:T(8,128)(2,1)S(1)} %get-tuple-element.42), kind=kOutput, calls=%fused_computation.30 | convolution fusion | flops 4831838208 | bytes 11796480 | tf_op jit(solution)/shard_map/srlh,lhjd->sjrd/dot_general | solution.py:100
  133.7 53.4 %all-to-all-done = bf16[128,24,1024]{2,1,0:T(8,128)(2,1)} async-done(((bf16[128,24,1024]{2,1,0:T(8,128)(2,1)}), bf16[128,24,1024]{2,1,0:T(8,128)(2,1)}, u32[]{:S(2)}, u32[]{:S(2)}) %all-to-all-start) | async-done | bytes 6291488 | tf_op jit(solution)/shard_map/all_to_all | solution.py:50
  187.1 9.4 %bitcast_convert_fusion = bf16[2,384,2,1024]{3,1,2,0:T(8,128)(2,1)} fusion(bf16[64,2,24,1024]{3,2,1,0:T(8,128)(2,1)} %bitcast.7, bf16[64,24,2,384]{3,1,2,0:T(8,128)(2,1)S(1)} %get-tuple-element.42), kind=kOutput, calls=%fused_computation.6 | convolution fusion | flops 4833411072 | bytes 11796480 | tf_op jit(solution)/shard_map/srlh,scrd->lhcd/dot_general | solution.py:119
  196.5 9.9 %multiply_convert_fusion.1 = (bf16[64,24,2,384]{3,1,2,0:T(8,128)(2,1)}, bf16[64,24,2,384]{3,1,2,0:T(8,128)(2,1)S(1)}) fusion(pred[24,2]{0,1:T(4,128)(4,1)S(1)} %iota_compare_fusion.4, f32[64,24,2,384,1]{3,1,4,2,0:T(8,128)S(1)} %copy-done.15, f32[64,24,2,384,1]{3,1,4,2,0:T(8,128)S(1)} %copy-done.16, bf16[2,48,2,8,1024]{4,3,2,1,0:T(8,128)(2,1)S(1)} %bitcast.213, ...), kind=kOutput, calls=%fused_computation.25 | convolution fusion | flops 4850712576 | bytes 23593008 | tf_op jit(solution)/shard_map/scrd,lhcd->srlh/dot_general | solution.py:122
  206.5 9.7 %all-to-all-start.2 = ((bf16[128,24,1024]{2,1,0:T(8,128)(2,1)}), bf16[128,24,1024]{2,1,0:T(8,128)(2,1)}, u32[]{:S(2)}, u32[]{:S(2)}) async-start(bf16[128,24,1024]{2,1,0:T(8,128)(2,1)} %bitcast.205), calls=%async_computation.2 | async-start | bytes 12582912 | tf_op jit(solution)/shard_map/all_to_all | solution.py:78
  216.2 4.6 %copy.97 = bf16[2,384,2,1024]{1,3,2,0:T(8,128)(2,1)} copy(bf16[2,384,2,1024]{3,1,2,0:T(8,128)(2,1)} %bitcast_convert_fusion) | data formatting | bytes 6291456 | tf_op jit(solution)/shard_map/convert_element_type | solution.py:121
  220.8 4.6 %copy.99 = bf16[2,384,2048]{2,1,0:T(8,128)(2,1)} copy(bf16[2,384,2048]{1,2,0:T(8,128)(2,1)} %bitcast.194) | data formatting | bytes 6291456
  225.4 9.3 %fusion.14 = bf16[2,2,1024,384]{2,3,1,0:T(8,128)(2,1)} fusion(bf16[64,2,24,1024]{3,2,1,0:T(8,128)(2,1)} %bitcast.199, bf16[64,24,2,384]{3,1,2,0:T(8,128)(2,1)S(1)} %get-tuple-element.41), kind=kOutput, calls=%fused_computation.32 | convolution fusion | flops 4833411072 | bytes 11796480 | tf_op jit(solution)/shard_map/scrd,srlh->lcdh/dot_general | solution.py:128
  234.7 4.6 %copy.91 = bf16[2,2,1024,384]{3,2,1,0:T(8,128)(2,1)} copy(bf16[2,2,1024,384]{2,3,1,0:T(8,128)(2,1)} %fusion.14) | data formatting | bytes 6291456 | tf_op jit(solution)/shard_map/convert_element_type | solution.py:130
  239.4 7.2 %fusion.19 = f32[64,24,2,1024,1]{3,1,4,2,0:T(8,128)S(1)} fusion(bf16[2,2,1024,384]{3,2,1,0:T(8,128)(2,1)} %bitcast.214, bf16[64,24,2,384]{3,1,2,0:T(8,128)(2,1)S(1)} %get-tuple-element.41), kind=kOutput, calls=%fused_computation.39 | convolution fusion | flops 4831838208 | bytes 18087936 | tf_op jit(solution)/shard_map/srlh,ljdh->sjrd/dot_general | solution.py:135
  246.6 7.5 %fusion = bf16[64,24,2,1024]{3,1,2,0:T(8,128)(2,1)} fusion(f32[64,24,2,1024,1]{3,1,4,2,0:T(8,128)S(1)} %fusion.19, bf16[2,2,1024,384]{3,2,1,0:T(8,128)(2,1)S(1)} %bitcast.217, bf16[64,24,2,384]{3,1,2,0:T(8,128)(2,1)S(1)} %copy-done.12), kind=kOutput, calls=%fused_computation.1 | convolution fusion | flops 4838129664 | bytes 24379392 | tf_op jit(solution)/shard_map/srlh,ljdh->sjrd/dot_general | solution.py:136
  254.1 42.9 %all-to-all-done.2 = bf16[128,24,1024]{2,1,0:T(8,128)(2,1)} async-done(((bf16[128,24,1024]{2,1,0:T(8,128)(2,1)}), bf16[128,24,1024]{2,1,0:T(8,128)(2,1)}, u32[]{:S(2)}, u32[]{:S(2)}) %all-to-all-start.2) | async-done | bytes 6291488 | tf_op jit(solution)/shard_map/all_to_all | solution.py:78
  297.0 10.0 %all-to-all-start.3 = ((bf16[128,24,1024]{2,1,0:T(8,128)(2,1)}), bf16[128,24,1024]{2,1,0:T(8,128)(2,1)}, u32[]{:S(2)}, u32[]{:S(2)}) async-start(bf16[128,24,1024]{2,1,0:T(8,128)(2,1)} %bitcast.204), calls=%async_computation.3 | async-start | bytes 12582912 | tf_op jit(solution)/shard_map/all_to_all | solution.py:78
  307.1 9.3 %fusion.15 = bf16[2,2,1024,384]{2,3,1,0:T(8,128)(2,1)} fusion(bf16[64,2,24,1024]{3,2,1,0:T(8,128)(2,1)} %bitcast.200, bf16[64,24,2,384]{3,1,2,0:T(8,128)(2,1)S(1)} %copy-done.13), kind=kOutput, calls=%fused_computation.33 | convolution fusion | flops 4833411072 | bytes 11796480 | tf_op jit(solution)/shard_map/scrd,srlh->lcdh/dot_general | solution.py:131
  316.4 4.7 %copy.94 = bf16[2,2,1024,384]{3,2,1,0:T(8,128)(2,1)} copy(bf16[2,2,1024,384]{2,3,1,0:T(8,128)(2,1)} %fusion.15) | data formatting | bytes 6291456 | tf_op jit(solution)/shard_map/convert_element_type | solution.py:133
  321.1 4.6 %fusion.53 = f32[3072,128]{1,0:T(8,128)S(1)} fusion(bf16[3072,1024]{1,0:T(8,128)(2,1)} %bitcast.28, bf16[128,1024]{1,0:T(8,128)(2,1)S(1)} %copy-done.6), kind=kOutput, calls=%fused_computation.76 | convolution fusion | flops 805306368 | bytes 8126464 | tf_op jit(solution)/shard_map/dot_general | solution.py:113
  326.1 1.9 broadcast_in_dim.92
  328.1 4.7 %fusion.41 = f32[256,1024]{1,0:T(8,128)S(1)} fusion(bf16[3072,1024]{1,0:T(8,128)(2,1)} %bitcast.28, bf16[384,8,2,128]{3,2,1,0:T(2,128)(2,1)S(1)} %bitcast.193), kind=kOutput, calls=%fused_computation.49 | convolution fusion | flops 1610612736 | bytes 8912896 | tf_op jit(solution)/shard_map/dot_general | solution.py:107
  334.4 56.5 %psum.7 = f32[128,8]{1,0:T(8,128)S(1)} all-reduce(f32[128,8]{1,0:T(8,128)S(1)} %select_reduce_fusion.2), channel_id=1, replica_groups=mesh['dp'=64,'col'=2] {'col'}, use_global_device_ids=true, to_apply=%region_8.9 | all-reduce | flops 1024 | bytes 8192 | tf_op jit(solution)/shard_map/psum | solution.py:140
  391.7 4.5 %convolution_convert_fusion.1 = bf16[128,1024]{1,0:T(8,128)(2,1)} fusion(bf16[128,3072]{0,1:T(8,128)(2,1)S(1)} %bitcast.207, bf16[3072,1024]{1,0:T(8,128)(2,1)} %bitcast.53), kind=kOutput, calls=%fused_computation.52 | convolution fusion | flops 805437440 | bytes 7340032 | tf_op jit(solution)/shard_map/dot_general | solution.py:88
  (68 shorter events, 7.1 us)
Async XLA Ops:
  0.6 9.3 %copy-start = (bf16[128,2048]{1,0:T(8,128)(2,1)S(1)}, bf16[128,2048]{1,0:T(8,128)(2,1)}, u32[]{:S(2)}) copy-start(bf16[128,2048]{1,0:T(8,128)(2,1)} %param.7) | copy-start | bytes 1572868
  0.6 10.3 %copy-start.5 = (bf16[128,1024]{1,0:T(8,128)(2,1)S(1)}, bf16[128,1024]{1,0:T(8,128)(2,1)}, u32[]{:S(2)}) copy-start(bf16[128,1024]{1,0:T(8,128)(2,1)} %param.13) | copy-start | bytes 786436
  4.3 11.1 %copy-start.3 = (s32[128,8]{1,0:T(8,128)}, s32[128,8]{1,0:T(8,128)S(1)}, u32[]{:S(2)}) copy-start(s32[128,8]{1,0:T(8,128)S(1)} %copy.79) | copy-start | bytes 12292
  96.6 90.5 %all-to-all-start = ((bf16[128,24,1024]{2,1,0:T(8,128)(2,1)}), bf16[128,24,1024]{2,1,0:T(8,128)(2,1)}, u32[]{:S(2)}, u32[]{:S(2)}) async-start(bf16[128,24,1024]{2,1,0:T(8,128)(2,1)} %bitcast.191), calls=%async_computation | async-start | bytes 12582912 | tf_op jit(solution)/shard_map/all_to_all | solution.py:50
  109.5 1.9 copy-start.9
  109.7 9.5 %slice-start = ((s8[6291456]{0:T(1024)(128)(4,1)}), s8[4194304]{0:T(1024)(128)(4,1)S(1)}, s32[]{:S(2)}) async-start(s8[6291456]{0:T(1024)(128)(4,1)} %bitcast.201), calls=%async_computation.4 | async-start | bytes 8388608
  111.5 7.7 %slice-start.1 = ((s8[6291456]{0:T(1024)(128)(4,1)}), s8[2097152]{0:T(1024)(128)(4,1)S(1)}, s32[]{:S(2)}) async-start(s8[6291456]{0:T(1024)(128)(4,1)} %bitcast.201), calls=%async_computation.5 | async-start | bytes 4194304
  111.5 7.7 %copy-start.10 = (bf16[2,2048,384]{2,1,0:T(8,128)(2,1)S(1)}, bf16[2,2048,384]{2,1,0:T(8,128)(2,1)}, u32[]{:S(2)}) copy-start(bf16[2,2048,384]{2,1,0:T(8,128)(2,1)} %param.11) | copy-start | bytes 9437188
  119.2 7.4 %copy-start.14 = (f32[64,24,2,384,1]{3,1,4,2,0:T(8,128)}, f32[64,24,2,384,1]{3,1,4,2,0:T(8,128)S(1)}, u32[]{:S(2)}) copy-start(f32[64,24,2,384,1]{3,1,4,2,0:T(8,128)S(1)} %fusion.52) | copy-start | bytes 14155780
  119.2 7.4 %copy-start.7 = (bf16[2,384,2048]{2,1,0:T(8,128)(2,1)S(1)}, bf16[2,384,2048]{2,1,0:T(8,128)(2,1)}, u32[]{:S(2)}) copy-start(bf16[2,384,2048]{2,1,0:T(8,128)(2,1)} %param.12) | copy-start | bytes 9437188
  187.1 9.4 %copy-start.8 = (bf16[2,384,2048]{2,1,0:T(8,128)(2,1)S(1)}, bf16[2,384,2048]{2,1,0:T(8,128)(2,1)}, u32[]{:S(2)}) copy-start(bf16[2,384,2048]{2,1,0:T(8,128)(2,1)} %param.12) | copy-start | bytes 9437188
  187.1 9.4 %copy-start.15 = (f32[64,24,2,384,1]{3,1,4,2,0:T(8,128)S(1)}, f32[64,24,2,384,1]{3,1,4,2,0:T(8,128)}, u32[]{:S(2)}) copy-start(f32[64,24,2,384,1]{3,1,4,2,0:T(8,128)} %copy-done.14) | copy-start | bytes 14155780
  187.1 9.4 %copy-start.16 = (f32[64,24,2,384,1]{3,1,4,2,0:T(8,128)S(1)}, f32[64,24,2,384,1]{3,1,4,2,0:T(8,128)}, u32[]{:S(2)}) copy-start(f32[64,24,2,384,1]{3,1,4,2,0:T(8,128)} %get-tuple-element.43) | copy-start | bytes 14155780
  206.5 90.6 %all-to-all-start.2 = ((bf16[128,24,1024]{2,1,0:T(8,128)(2,1)}), bf16[128,24,1024]{2,1,0:T(8,128)(2,1)}, u32[]{:S(2)}, u32[]{:S(2)}) async-start(bf16[128,24,1024]{2,1,0:T(8,128)(2,1)} %bitcast.205), calls=%async_computation.2 | async-start | bytes 12582912 | tf_op jit(solution)/shard_map/all_to_all | solution.py:78
  239.3 7.2 %copy-start.11 = (bf16[2,2048,384]{2,1,0:T(8,128)(2,1)S(1)}, bf16[2,2048,384]{2,1,0:T(8,128)(2,1)}, u32[]{:S(2)}) copy-start(bf16[2,2048,384]{2,1,0:T(8,128)(2,1)} %param.11) | copy-start | bytes 9437188
  239.3 7.3 %copy-start.12 = (bf16[64,24,2,384]{3,1,2,0:T(8,128)(2,1)S(1)}, bf16[64,24,2,384]{3,1,2,0:T(8,128)(2,1)}, u32[]{:S(2)}) copy-start(bf16[64,24,2,384]{3,1,2,0:T(8,128)(2,1)} %get-tuple-element.40) | copy-start | bytes 7077892
  297.0 10.1 %copy-start.13 = (bf16[64,24,2,384]{3,1,2,0:T(8,128)(2,1)S(1)}, bf16[64,24,2,384]{3,1,2,0:T(8,128)(2,1)}, u32[]{:S(2)}) copy-start(bf16[64,24,2,384]{3,1,2,0:T(8,128)(2,1)} %get-tuple-element.40) | copy-start | bytes 7077892
  297.0 94.5 %all-to-all-start.3 = ((bf16[128,24,1024]{2,1,0:T(8,128)(2,1)}), bf16[128,24,1024]{2,1,0:T(8,128)(2,1)}, u32[]{:S(2)}, u32[]{:S(2)}) async-start(bf16[128,24,1024]{2,1,0:T(8,128)(2,1)} %bitcast.204), calls=%async_computation.3 | async-start | bytes 12582912 | tf_op jit(solution)/shard_map/all_to_all | solution.py:78
  316.4 4.7 %copy-start.6 = (bf16[128,1024]{1,0:T(8,128)(2,1)S(1)}, bf16[128,1024]{1,0:T(8,128)(2,1)}, u32[]{:S(2)}) copy-start(bf16[128,1024]{1,0:T(8,128)(2,1)} %param.13) | copy-start | bytes 786436
  328.1 5.5 %copy-start.4 = (s32[128,8]{1,0:T(8,128)S(1)}, s32[128,8]{1,0:T(8,128)}, u32[]{:S(2)}) copy-start(s32[128,8]{1,0:T(8,128)} %copy-done.3) | copy-start | bytes 12292
  328.1 63.5 %copy-start.2 = (bf16[128,1536]{0,1:T(8,128)(2,1)S(1)}, bf16[128,1536]{0,1:T(8,128)(2,1)}, u32[]{:S(2)}) copy-start(bf16[128,1536]{0,1:T(8,128)(2,1)} %copy.85) | copy-start | bytes 1179652
  332.8 63.5 %copy-start.1 = (bf16[128,2048]{1,0:T(8,128)(2,1)S(1)}, bf16[128,2048]{1,0:T(8,128)(2,1)}, u32[]{:S(2)}) copy-start(bf16[128,2048]{1,0:T(8,128)(2,1)} %param.7) | copy-start | bytes 1572868

commit v4 on v3

--- a/solution.py
+++ b/solution.py
@@ -73,8 +73,10 @@
             (tok_count, owners, cols, rows_per_owner),
         )
 
-    def send_back(part):
-        part = part.astype(jnp.bfloat16)
+    def send_back(halves):
+        if isinstance(halves, list):
+            halves = jnp.stack(halves, axis=1)
+        part = halves.astype(jnp.bfloat16)
         got = lax.all_to_all(
             part.reshape(owners * cols, rows_per_owner, half_width), both, 0, 0, tiled=True
         )
@@ -97,7 +99,10 @@
     sigmoid_g = jax.nn.sigmoid(gate_acts)
     silu_g = gate_acts * sigmoid_g
     hidden = (silu_g * up_acts).astype(jnp.bfloat16)
-    out_halves = jnp.einsum("srlh,lhjd->sjrd", hidden, w_down_h, preferred_element_type=jnp.float32)
+    out_halves = [
+        jnp.einsum("srlh,lhd->srd", hidden, w, preferred_element_type=jnp.float32)
+        for w in halves_of(w_down, 2)
+    ]
     d_out, out_halves = lax.optimization_barrier((d_out, out_halves))
     got_out = send_back(out_halves)
     stacked = jnp.broadcast_to(

time: 404 us -> 390 us (0.965)
  waiting for transfers between devices: 96.3 us -> 70 us
  local copies, waits for them, and re-layouts: 31.1 us -> 36.4 us
    all_to_all x2, waiting for transfers between devices: 42.9 us -> 17.6 us  [send_back(): lax.all_to_all(part.reshape(owners * cols, rows_per_owner, half_width), b...]
    dot_general x1, matrix products: 9.95 us -> 14.8 us  [body(): jnp.einsum('scrd,lhcd->srlh', d_out, w_down_h, preferred_element_type=jnp...]
    unnamed x42 -> x44, local copies, waits for them, and re-layouts: 7.03 us -> 8.6 us
  transfers between devices with their start and end apart: 3 -> 3, of which waited for: 2 -> 2; matrix products, arithmetic and copies ran while one was open for 23% -> 30% of each run, Pallas kernels for 0% -> 0%
where the time goes in v4:
time: 390 us; the launch traced here: 382 us
  blocking collectives  137 us (35%)
  matrix products  93.6 us (24%)
  waiting for transfers between devices  70 us (18%)
  local copies, waits for them, and re-layouts  36.4 us (9%)
  starting transfers between devices  31.9 us (8%)
  other arithmetic  12.4 us (3%)
    all_to_all x1, blocking collectives, dispatch(): got = lax.all_to_all(sent, both, 0, 0, tiled=True)  80.2 us
    psum x1, blocking collectives, body(): grad_probs = lax.psum(prob_part, 'col')  56.5 us
    all_to_all x1, waiting for transfers between devices, dispatch(): got = lax.all_to_all(sent, both, 0, 0, tiled=True)  52.4 us
    all_to_all x2, starting transfers between devices, send_back(): lax.all_to_all(part.reshape(owners * cols, rows_per_owner, half_width), b...  20.4 us
    all_to_all x2, waiting for transfers between devices, send_back(): lax.all_to_all(part.reshape(owners * cols, rows_per_owner, half_width), b...  17.6 us
    dot_general x1, matrix products, body(): jnp.einsum('scrd,lhcd->srlh', d_out, w_down_h, preferred_element_type=jnp...  14.8 us
    all_to_all x1, starting transfers between devices, dispatch(): got = lax.all_to_all(sent, both, 0, 0, tiled=True)  11.5 us
    dot_general x1, matrix products, body(): jnp.einsum('scrd,srlh->lcdh', row_block, d_up, preferred_element_type=jnp...  9.3 us
  transfers between devices with their start and end apart: 3, of which 2 were waited for; matrix products, arithmetic and copies ran while one was open for 30% of the time, Pallas kernels for 0%

profile of v4, /device:TPU:82, one launch (start us, length us, event | category | flops | bytes accessed | tf_op | source)
XLA Modules:
  0.0 382.2 jit_solution(657539772754310861)
XLA Ops:
  4.3 3.1 fusion.10
  7.5 2.5 select_reduce_fusion
  12.1 3.4 broadcast_in_dim.86
  16.4 80.2 %all_to_all.20 = bf16[128,24,1024]{2,1,0:T(8,128)(2,1)} all-to-all(bf16[128,24,1024]{2,1,0:T(8,128)(2,1)S(1)} %bitcast.196), channel_id=1, replica_groups=mesh['dp'=64,'col'=2] {'dp','col'}, dimensions={0} | all-to-all | bytes 12582912 | tf_op jit(solution)/shard_map/all_to_all | solution.py:50
  96.6 11.5 %all-to-all-start = ((bf16[128,24,1024]{2,1,0:T(8,128)(2,1)}), bf16[128,24,1024]{2,1,0:T(8,128)(2,1)}, u32[]{:S(2)}, u32[]{:S(2)}) async-start(bf16[128,24,1024]{2,1,0:T(8,128)(2,1)} %bitcast.194), calls=%async_computation | async-start | bytes 12582912 | tf_op jit(solution)/shard_map/all_to_all | solution.py:50
  109.6 1.7 copy.83
  111.4 7.7 %fusion.54 = f32[64,24,2,384,1]{3,1,4,2,0:T(8,128)S(1)} fusion(bf16[64,2,24,1024,1]{3,2,1,4,0:T(8,128)(2,1)} %bitcast.202, bf16[2,2,1024,384,1]{3,2,1,0,4:T(8,128)(2,1)S(1)} %bitcast.221), kind=kOutput, calls=%fused_computation.80 | convolution fusion | flops 4831838208 | bytes 14155776 | tf_op jit(solution)/shard_map/scrd,lcdh->srlh/dot_general | solution.py:95
  119.1 7.4 %multiply_convert_fusion.3 = (bf16[64,24,2,384]{3,1,2,0:T(8,128)(2,1)S(1)}, f32[64,24,2,384,1]{3,1,4,2,0:T(8,128)}) fusion(pred[24,2]{0,1:T(4,128)(4,1)S(1)} %iota_compare_fusion.4, f32[64,24,2,384,1]{3,1,4,2,0:T(8,128)S(1)} %fusion.54, bf16[64,2,24,1024,1]{3,2,1,4,0:T(8,128)(2,1)S(1)} %bitcast.206, bf16[2,2,1024,384,1]{3,2,1,0,4:T(8,128)(2,1)S(1)} %bitcast.222), kind=kOutput, calls=%fused_computation.28 | convolution fusion | flops 4841275392 | bytes 21233712 | tf_op jit(solution)/shard_map/scrd,lcdh->srlh/dot_general | solution.py:96
  126.5 4.0 %convolution_bitcast_fusion = bf16[64,24,1024]{2,1,0:T(8,128)(2,1)} fusion(bf16[64,24,2,384]{3,1,2,0:T(8,128)(2,1)S(1)} %get-tuple-element.44, bf16[2,384,2048]{2,1,0:T(8,128)(2,1)S(1)} %copy-done.7), kind=kOutput, calls=%fused_computation.43 | convolution fusion | flops 2415919104 | bytes 7077888 | tf_op jit(solution)/shard_map/srlh,lhd->srd/dot_general | solution.py:103
  130.5 4.0 %convolution_bitcast_fusion.1 = bf16[64,24,1024]{2,1,0:T(8,128)(2,1)} fusion(bf16[64,24,2,384]{3,1,2,0:T(8,128)(2,1)S(1)} %get-tuple-element.44, bf16[2,384,2048]{2,1,0:T(8,128)(2,1)S(1)} %copy-done.7), kind=kOutput, calls=%fused_computation.44 | convolution fusion | flops 2415919104 | bytes 7077888 | tf_op jit(solution)/shard_map/srlh,lhd->srd/dot_general | solution.py:103
  134.5 52.4 %all-to-all-done = bf16[128,24,1024]{2,1,0:T(8,128)(2,1)} async-done(((bf16[128,24,1024]{2,1,0:T(8,128)(2,1)}), bf16[128,24,1024]{2,1,0:T(8,128)(2,1)}, u32[]{:S(2)}, u32[]{:S(2)}) %all-to-all-start) | async-done | bytes 6291488 | tf_op jit(solution)/shard_map/all_to_all | solution.py:50
  186.9 3.4 pad_maximum_fusion
  190.3 3.3 copy.80
  193.7 10.3 %all-to-all-start.2 = ((bf16[128,24,1024]{2,1,0:T(8,128)(2,1)}), bf16[128,24,1024]{2,1,0:T(8,128)(2,1)}, u32[]{:S(2)}, u32[]{:S(2)}) async-start(bf16[128,24,1024]{2,1,0:T(8,128)(2,1)} %bitcast.195), calls=%async_computation.2 | async-start | bytes 12582912 | tf_op jit(solution)/shard_map/all_to_all | solution.py:80
  204.0 9.3 %bitcast_convert_fusion = bf16[2,384,2,1024]{3,1,2,0:T(8,128)(2,1)} fusion(bf16[64,2,24,1024]{3,2,1,0:T(8,128)(2,1)} %bitcast.7, bf16[64,24,2,384]{3,1,2,0:T(8,128)(2,1)S(1)} %get-tuple-element.44), kind=kOutput, calls=%fused_computation.7 | convolution fusion | flops 4833411072 | bytes 11796480 | tf_op jit(solution)/shard_map/srlh,scrd->lhcd/dot_general | solution.py:124
  213.3 4.6 %copy.96 = bf16[2,384,2,1024]{1,3,2,0:T(8,128)(2,1)} copy(bf16[2,384,2,1024]{3,1,2,0:T(8,128)(2,1)} %bitcast_convert_fusion) | data formatting | bytes 6291456 | tf_op jit(solution)/shard_map/convert_element_type | solution.py:126
  217.9 4.8 %copy.98 = bf16[2,384,2048]{2,1,0:T(8,128)(2,1)} copy(bf16[2,384,2048]{1,2,0:T(8,128)(2,1)} %bitcast.198) | data formatting | bytes 6291456
  222.7 14.8 %multiply_convert_fusion.1 = (bf16[64,24,2,384]{3,1,2,0:T(8,128)(2,1)}, bf16[64,24,2,384]{3,1,2,0:T(8,128)(2,1)S(1)}) fusion(pred[24,2]{0,1:T(4,128)(4,1)S(1)} %iota_compare_fusion.4, f32[64,24,2,384,1]{3,1,4,2,0:T(8,128)} %copy-done.15, f32[64,24,2,384,1]{3,1,4,2,0:T(8,128)} %get-tuple-element.45, bf16[2,48,2,8,1024]{4,3,2,1,0:T(8,128)(2,1)} %bitcast.219, ...), kind=kOutput, calls=%fused_computation.26 | convolution fusion | flops 4850712576 | bytes 23593008 | tf_op jit(solution)/shard_map/scrd,lhcd->srlh/dot_general | solution.py:127
  237.5 1.4 copy-done.11
  238.9 6.5 %fusion.14 = bf16[2,2,1024,384]{2,3,1,0:T(8,128)(2,1)} fusion(bf16[64,2,24,1024]{3,2,1,0:T(8,128)(2,1)S(1)} %bitcast.209, bf16[64,24,2,384]{3,1,2,0:T(8,128)(2,1)S(1)} %get-tuple-element.43), kind=kOutput, calls=%fused_computation.32 | convolution fusion | flops 4833411072 | bytes 11796480 | tf_op jit(solution)/shard_map/scrd,srlh->lcdh/dot_general | solution.py:133
  245.4 4.9 %copy.90 = bf16[2,2,1024,384]{3,2,1,0:T(8,128)(2,1)} copy(bf16[2,2,1024,384]{2,3,1,0:T(8,128)(2,1)} %fusion.14) | data formatting | bytes 6291456 | tf_op jit(solution)/shard_map/convert_element_type | solution.py:135
  250.4 7.2 %fusion.18 = f32[64,24,2,1024,1]{3,1,4,2,0:T(8,128)S(1)} fusion(bf16[2,2,1024,384]{3,2,1,0:T(8,128)(2,1)} %bitcast.220, bf16[64,24,2,384]{3,1,2,0:T(8,128)(2,1)S(1)} %copy-done.12), kind=kOutput, calls=%fused_computation.37 | convolution fusion | flops 4831838208 | bytes 18087936 | tf_op jit(solution)/shard_map/srlh,ljdh->sjrd/dot_general | solution.py:140
  257.6 7.6 %fusion = bf16[64,24,2,1024]{3,1,2,0:T(8,128)(2,1)} fusion(f32[64,24,2,1024,1]{3,1,4,2,0:T(8,128)S(1)} %fusion.18, bf16[2,2,1024,384]{3,2,1,0:T(8,128)(2,1)S(1)} %bitcast.223, bf16[64,24,2,384]{3,1,2,0:T(8,128)(2,1)S(1)} %copy-done.13), kind=kOutput, calls=%fused_computation.1 | convolution fusion | flops 4838129664 | bytes 24379392 | tf_op jit(solution)/shard_map/srlh,ljdh->sjrd/dot_general | solution.py:141
  265.2 17.6 %all-to-all-done.2 = bf16[128,24,1024]{2,1,0:T(8,128)(2,1)} async-done(((bf16[128,24,1024]{2,1,0:T(8,128)(2,1)}), bf16[128,24,1024]{2,1,0:T(8,128)(2,1)}, u32[]{:S(2)}, u32[]{:S(2)}) %all-to-all-start.2) | async-done | bytes 6291488 | tf_op jit(solution)/shard_map/all_to_all | solution.py:80
  282.8 10.0 %all-to-all-start.3 = ((bf16[128,24,1024]{2,1,0:T(8,128)(2,1)}), bf16[128,24,1024]{2,1,0:T(8,128)(2,1)}, u32[]{:S(2)}, u32[]{:S(2)}) async-start(bf16[128,24,1024]{2,1,0:T(8,128)(2,1)} %bitcast.210), calls=%async_computation.3 | async-start | bytes 12582912 | tf_op jit(solution)/shard_map/all_to_all | solution.py:80
  292.8 9.3 %fusion.15 = bf16[2,2,1024,384]{2,3,1,0:T(8,128)(2,1)} fusion(bf16[64,2,24,1024]{3,2,1,0:T(8,128)(2,1)} %bitcast.203, bf16[64,24,2,384]{3,1,2,0:T(8,128)(2,1)S(1)} %copy-done.14), kind=kOutput, calls=%fused_computation.33 | convolution fusion | flops 4833411072 | bytes 11796480 | tf_op jit(solution)/shard_map/scrd,srlh->lcdh/dot_general | solution.py:136
  302.1 4.7 %copy.93 = bf16[2,2,1024,384]{3,2,1,0:T(8,128)(2,1)} copy(bf16[2,2,1024,384]{2,3,1,0:T(8,128)(2,1)} %fusion.15) | data formatting | bytes 6291456 | tf_op jit(solution)/shard_map/convert_element_type | solution.py:138
  306.8 4.6 %fusion.55 = f32[3072,128]{1,0:T(8,128)S(1)} fusion(bf16[3072,1024]{1,0:T(8,128)(2,1)} %bitcast.30, bf16[128,1024]{1,0:T(8,128)(2,1)S(1)} %copy-done.6), kind=kOutput, calls=%fused_computation.81 | convolution fusion | flops 805306368 | bytes 8126464 | tf_op jit(solution)/shard_map/dot_general | solution.py:118
  311.8 1.9 broadcast_in_dim.92
  313.8 4.7 %fusion.39 = f32[256,1024]{1,0:T(8,128)S(1)} fusion(bf16[3072,1024]{1,0:T(8,128)(2,1)} %bitcast.30, bf16[384,8,2,128]{3,2,1,0:T(2,128)(2,1)S(1)} %bitcast.197), kind=kOutput, calls=%fused_computation.50 | convolution fusion | flops 1610612736 | bytes 8912896 | tf_op jit(solution)/shard_map/dot_general | solution.py:112
  320.2 56.5 %psum.7 = f32[128,8]{1,0:T(8,128)S(1)} all-reduce(f32[128,8]{1,0:T(8,128)S(1)} %select_reduce_fusion.2), channel_id=1, replica_groups=mesh['dp'=64,'col'=2] {'col'}, use_global_device_ids=true, to_apply=%region_8.9 | all-reduce | flops 1024 | bytes 8192 | tf_op jit(solution)/shard_map/psum | solution.py:145
  377.4 4.5 %convolution_convert_fusion.1 = bf16[128,1024]{1,0:T(8,128)(2,1)} fusion(bf16[128,3072]{0,1:T(8,128)(2,1)S(1)} %bitcast.212, bf16[3072,1024]{1,0:T(8,128)(2,1)} %bitcast.55), kind=kOutput, calls=%fused_computation.57 | convolution fusion | flops 805437440 | bytes 7340032 | tf_op jit(solution)/shard_map/dot_general | solution.py:90
  (74 shorter events, 11.0 us)
Async XLA Ops:
  0.6 9.3 %copy-start = (bf16[128,2048]{1,0:T(8,128)(2,1)S(1)}, bf16[128,2048]{1,0:T(8,128)(2,1)}, u32[]{:S(2)}) copy-start(bf16[128,2048]{1,0:T(8,128)(2,1)} %param.7) | copy-start | bytes 1572868
  0.6 10.3 %copy-start.5 = (bf16[128,1024]{1,0:T(8,128)(2,1)S(1)}, bf16[128,1024]{1,0:T(8,128)(2,1)}, u32[]{:S(2)}) copy-start(bf16[128,1024]{1,0:T(8,128)(2,1)} %param.13) | copy-start | bytes 786436
  4.3 11.2 %copy-start.3 = (s32[128,8]{1,0:T(8,128)}, s32[128,8]{1,0:T(8,128)S(1)}, u32[]{:S(2)}) copy-start(s32[128,8]{1,0:T(8,128)S(1)} %copy.78) | copy-start | bytes 12292
  96.6 90.3 %all-to-all-start = ((bf16[128,24,1024]{2,1,0:T(8,128)(2,1)}), bf16[128,24,1024]{2,1,0:T(8,128)(2,1)}, u32[]{:S(2)}, u32[]{:S(2)}) async-start(bf16[128,24,1024]{2,1,0:T(8,128)(2,1)} %bitcast.194), calls=%async_computation | async-start | bytes 12582912 | tf_op jit(solution)/shard_map/all_to_all | solution.py:50
  109.4 2.0 copy-start.8
  109.6 9.5 %slice-start = ((s8[6291456]{0:T(1024)(128)(4,1)}), s8[4194304]{0:T(1024)(128)(4,1)S(1)}, s32[]{:S(2)}) async-start(s8[6291456]{0:T(1024)(128)(4,1)} %bitcast.204), calls=%async_computation.4 | async-start | bytes 8388608
  111.3 7.7 %slice-start.1 = ((s8[6291456]{0:T(1024)(128)(4,1)}), s8[2097152]{0:T(1024)(128)(4,1)S(1)}, s32[]{:S(2)}) async-start(s8[6291456]{0:T(1024)(128)(4,1)} %bitcast.204), calls=%async_computation.5 | async-start | bytes 4194304
  111.4 7.7 %copy-start.9 = (bf16[2,2048,384]{2,1,0:T(8,128)(2,1)S(1)}, bf16[2,2048,384]{2,1,0:T(8,128)(2,1)}, u32[]{:S(2)}) copy-start(bf16[2,2048,384]{2,1,0:T(8,128)(2,1)} %param.11) | copy-start | bytes 9437188
  119.1 7.5 %copy-start.15 = (f32[64,24,2,384,1]{3,1,4,2,0:T(8,128)}, f32[64,24,2,384,1]{3,1,4,2,0:T(8,128)S(1)}, u32[]{:S(2)}) copy-start(f32[64,24,2,384,1]{3,1,4,2,0:T(8,128)S(1)} %fusion.54) | copy-start | bytes 14155780
  119.1 7.4 %copy-start.7 = (bf16[2,384,2048]{2,1,0:T(8,128)(2,1)S(1)}, bf16[2,384,2048]{2,1,0:T(8,128)(2,1)}, u32[]{:S(2)}) copy-start(bf16[2,384,2048]{2,1,0:T(8,128)(2,1)} %param.12) | copy-start | bytes 9437188
  193.7 89.1 %all-to-all-start.2 = ((bf16[128,24,1024]{2,1,0:T(8,128)(2,1)}), bf16[128,24,1024]{2,1,0:T(8,128)(2,1)}, u32[]{:S(2)}, u32[]{:S(2)}) async-start(bf16[128,24,1024]{2,1,0:T(8,128)(2,1)} %bitcast.195), calls=%async_computation.2 | async-start | bytes 12582912 | tf_op jit(solution)/shard_map/all_to_all | solution.py:80
  217.9 21.0 %slice-start.2 = ((s8[6291456]{0:T(1024)(128)(4,1)}), s8[2097152]{0:T(1024)(128)(4,1)S(1)}, s32[]{:S(2)}) async-start(s8[6291456]{0:T(1024)(128)(4,1)} %bitcast.207), calls=%async_computation.6 | async-start | bytes 4194304
  222.7 16.2 %slice-start.3 = ((s8[6291456]{0:T(1024)(128)(4,1)}), s8[4194304]{0:T(1024)(128)(4,1)S(1)}, s32[]{:S(2)}) async-start(s8[6291456]{0:T(1024)(128)(4,1)} %bitcast.207), calls=%async_computation.7 | async-start | bytes 8388608
  237.5 1.4 copy-start.11
  245.4 4.9 %copy-start.12 = (bf16[64,24,2,384]{3,1,2,0:T(8,128)(2,1)S(1)}, bf16[64,24,2,384]{3,1,2,0:T(8,128)(2,1)}, u32[]{:S(2)}) copy-start(bf16[64,24,2,384]{3,1,2,0:T(8,128)(2,1)} %copy-done.11) | copy-start | bytes 7077892
  250.3 7.3 %copy-start.10 = (bf16[2,2048,384]{2,1,0:T(8,128)(2,1)S(1)}, bf16[2,2048,384]{2,1,0:T(8,128)(2,1)}, u32[]{:S(2)}) copy-start(bf16[2,2048,384]{2,1,0:T(8,128)(2,1)} %param.11) | copy-start | bytes 9437188
  250.4 7.3 %copy-start.13 = (bf16[64,24,2,384]{3,1,2,0:T(8,128)(2,1)S(1)}, bf16[64,24,2,384]{3,1,2,0:T(8,128)(2,1)}, u32[]{:S(2)}) copy-start(bf16[64,24,2,384]{3,1,2,0:T(8,128)(2,1)} %get-tuple-element.42) | copy-start | bytes 7077892
  282.8 10.1 %copy-start.14 = (bf16[64,24,2,384]{3,1,2,0:T(8,128)(2,1)S(1)}, bf16[64,24,2,384]{3,1,2,0:T(8,128)(2,1)}, u32[]{:S(2)}) copy-start(bf16[64,24,2,384]{3,1,2,0:T(8,128)(2,1)} %get-tuple-element.42) | copy-start | bytes 7077892
  282.8 94.5 %all-to-all-start.3 = ((bf16[128,24,1024]{2,1,0:T(8,128)(2,1)}), bf16[128,24,1024]{2,1,0:T(8,128)(2,1)}, u32[]{:S(2)}, u32[]{:S(2)}) async-start(bf16[128,24,1024]{2,1,0:T(8,128)(2,1)} %bitcast.210), calls=%async_computation.3 | async-start | bytes 12582912 | tf_op jit(solution)/shard_map/all_to_all | solution.py:80
  302.1 4.7 %copy-start.6 = (bf16[128,1024]{1,0:T(8,128)(2,1)S(1)}, bf16[128,1024]{1,0:T(8,128)(2,1)}, u32[]{:S(2)}) copy-start(bf16[128,1024]{1,0:T(8,128)(2,1)} %param.13) | copy-start | bytes 786436
  313.8 5.5 %copy-start.4 = (s32[128,8]{1,0:T(8,128)S(1)}, s32[128,8]{1,0:T(8,128)}, u32[]{:S(2)}) copy-start(s32[128,8]{1,0:T(8,128)} %copy-done.3) | copy-start | bytes 12292
  313.8 63.5 %copy-start.2 = (bf16[128,1536]{0,1:T(8,128)(2,1)S(1)}, bf16[128,1536]{0,1:T(8,128)(2,1)}, u32[]{:S(2)}) copy-start(bf16[128,1536]{0,1:T(8,128)(2,1)} %copy.84) | copy-start | bytes 1179652
  318.5 63.5 %copy-start.1 = (bf16[128,2048]{1,0:T(8,128)(2,1)S(1)}, bf16[128,2048]{1,0:T(8,128)(2,1)}, u32[]{:S(2)}) copy-start(bf16[128,2048]{1,0:T(8,128)(2,1)} %param.7) | copy-start | bytes 1572868
